TPU v7x, 256 devices: a whole 4x4x8 slice. The times are simulated.
256 devices in a mesh: row: 16 (over y, x), col: 16 (over z, core).
Axes of the slice: x: 4, y: 4, z: 8, core: 2. Of those that a mesh axis runs over, the one named last changes fastest.
Arguments:
- fitting: bfloat16 [512, 512, 256], P(('row', 'col')), may hold values from -6 to 6
- coefficients: bfloat16 [64, 64, 6, 256, 128], P('row', 'col'), may hold values from -0.375 to 0.375
- amplitudes: bfloat16 [64, 64, 4096], P('row', 'col'), may hold values from -6 to 6
- intersections: bfloat16 [64, 64, 8, 4096], P('row', 'col'), may hold values from -0.33 to 1.33
- virtual_energy: float32 [64, 64, 64], P('row', 'col'), may hold values from 0.2 to 2
- occupied_energy: float32 [64], replicated, may hold values from -1.5 to -0.3
- kept_count: int32 [64, 64], P('row', 'col'), may hold values from 16 to 64
- orbital_atoms: int32 [64, 3], replicated, may hold values from 0 to 511, as said below
- fock_partner: int32 [64, 4], replicated, may hold values from 0 to 63, as said below
- fock_value: float32 [64, 4], replicated, may hold values from -3 to 3
Outputs:
- residual: float32 [64, 64, 4096], P('row', 'col')
Inputs may be any that keep to these rules, and one draw needn't show every extreme that they name: `orbital_atoms`: the 3 atoms of orbital i are different and lie in [(i // 4) * 32, (i // 4 + 1) * 32). fock_partner[i, n] differs from i by at most 4.
All inputs are finite; a program needn't handle non-finite values.
Results may differ from a plain program's by a relative error of at most 0.0029.
Values may be sent and summed in bfloat16 or wider, within the bound.
A program may use at most 128 MiB of HBM per device.

v0:
```python
import jax
import jax.numpy as jnp
from jax import lax
from jax.sharding import PartitionSpec as P

AUX = 512
NPNO = 64
DOMAIN = 3
PARTNERS = 4


def from_root(value, axis, source):
    kept = jnp.where(lax.axis_index(axis) == source, value, 0).astype(value.dtype)
    return lax.psum(kept, axis)


def passed_along(block, axis, distance):
    devices = range(lax.axis_size(axis))
    route = [(i - distance, i) for i in devices if i - distance in devices]
    return lax.ppermute(block, axis, route)


def on_device(
    fitting,
    coefficients,
    amplitudes,
    intersections,
    virtual_energy,
    occupied_energy,
    kept_count,
    orbital_atoms,
    fock_partner,
    fock_value,
):
    row_count = amplitudes.shape[0]
    column_count = amplitudes.shape[1]
    domain_size = orbital_atoms.shape[1]
    row_place = lax.axis_index("row")
    column_place = lax.axis_index("col")
    row_atoms = fitting.shape[0] * lax.axis_size("col")
    first_row = row_place * row_count
    first_column = column_place * column_count
    wanted = (
        lax.dynamic_slice_in_dim(orbital_atoms, first_row, row_count, 0) - row_place * row_atoms
    )
    piece = lax.all_gather(fitting, "col", axis=0, tiled=True)
    labels = jnp.arange(piece.shape[0], dtype=jnp.int32)
    picker = (wanted[:, :, None] == labels[None, None, :]).astype(jnp.bfloat16)
    added = jnp.einsum("ism,map->isap", picker, piece, preferred_element_type=jnp.float32)
    row_fit = added.astype(jnp.bfloat16)
    source_row = first_column // row_count
    column_fit = from_root(row_fit, "row", source_row)
    own_side = jnp.einsum(
        "isap,ijspq->ijsaq",
        row_fit,
        coefficients[:, :, :domain_size],
        preferred_element_type=jnp.float32,
    ).astype(jnp.bfloat16)
    other_side = jnp.einsum(
        "jsap,ijspq->ijsaq",
        column_fit,
        coefficients[:, :, domain_size:],
        preferred_element_type=jnp.float32,
    ).astype(jnp.bfloat16)
    exchange_part = jnp.einsum(
        "ijsaq,ijsar->ijqr",
        own_side[..., :NPNO],
        own_side[..., NPNO:],
        preferred_element_type=jnp.float32,
    )
    exchange_part = exchange_part + jnp.einsum(
        "ijsaq,ijsar->ijqr",
        other_side[..., :NPNO],
        other_side[..., NPNO:],
        preferred_element_type=jnp.float32,
    )
    exchange_part = exchange_part * (2 * DOMAIN * AUX) ** (-0.5)
    row_partner = lax.dynamic_slice_in_dim(fock_partner, first_row, row_count, 0)
    column_partner = lax.dynamic_slice_in_dim(fock_partner, first_column, column_count, 0)
    below_rows = passed_along(amplitudes, "row", 1)
    above_rows = passed_along(amplitudes, "row", -1)
    row_source = jnp.concatenate([below_rows, amplitudes, above_rows], axis=0)
    below_columns = passed_along(amplitudes, "col", 1)
    above_columns = passed_along(amplitudes, "col", -1)
    column_source = jnp.concatenate([below_columns, amplitudes, above_columns], axis=1)
    row_pick = row_partner - (first_row - column_count)
    column_pick = column_partner - (first_column - column_count)
    from_rows = jnp.transpose(jnp.take(row_source, row_pick, axis=0), (0, 2, 1, 3))
    from_columns = jnp.take(column_source, column_pick, axis=1)
    partners = jnp.concatenate([from_rows, from_columns], axis=2).reshape(
        row_count, column_count, 2 * PARTNERS, NPNO, NPNO
    )
    intersection_mats = intersections.reshape(row_count, column_count, 2 * PARTNERS, NPNO, NPNO)
    half = jnp.einsum(
        "ijnab,ijnbc->ijnac", intersection_mats, partners, preferred_element_type=jnp.float32
    ).astype(jnp.bfloat16)
    sandwich = jnp.einsum(
        "ijnac,ijndc->ijnad", half, intersection_mats, preferred_element_type=jnp.float32
    )
    row_weight = lax.dynamic_slice_in_dim(fock_value, first_row, row_count, 0)
    column_weight = lax.dynamic_slice_in_dim(fock_value, first_column, column_count, 0)
    weights = jnp.concatenate(
        [
            jnp.broadcast_to(row_weight[:, None, :], (row_count, column_count, PARTNERS)),
            jnp.broadcast_to(column_weight[None, :, :], (row_count, column_count, PARTNERS)),
        ],
        axis=2,
    )
    coupling = jnp.einsum("ijn,ijnad->ijad", weights, sandwich)
    row_occupied = lax.dynamic_slice_in_dim(occupied_energy, first_row, row_count, 0)
    column_occupied = lax.dynamic_slice_in_dim(occupied_energy, first_column, column_count, 0)
    shift = (
        virtual_energy[:, :, :, None]
        + virtual_energy[:, :, None, :]
        - row_occupied[:, None, None, None]
        - column_occupied[None, :, None, None]
    )
    current = amplitudes.reshape(row_count, column_count, NPNO, NPNO).astype(jnp.float32)
    result = exchange_part + shift * current - coupling
    levels = jnp.arange(NPNO, dtype=jnp.int32)
    count = kept_count[:, :, None, None]
    keep = (levels[None, None, :, None] < count) & (levels[None, None, None, :] < count)
    masked = jnp.where(keep, result, jnp.zeros_like(result))
    return masked.reshape(row_count, column_count, NPNO * NPNO)


def solution(mesh):
    placed = (
        P(("row", "col"), None, None),
        P("row", "col", None, None, None),
        P("row", "col", None),
        P("row", "col", None, None),
        P("row", "col", None),
        P(),
        P("row", "col"),
        P(),
        P(),
        P(),
    )
    return jax.shard_map(
        on_device, mesh=mesh, in_specs=placed, out_specs=P("row", "col", None), check_vma=False
    )
```

profile of v0, /device:TPU:1, one launch (start us, length us, event | category | flops | bytes accessed | tf_op | source)
XLA Modules:
  0.0 198.9 jit_solution(497864777100827050)
XLA Ops:
  7.3 1.0 copy.82
  8.3 4.9 %collective-permute-start.2 = (bf16[4,4,4096]{2,0,1:T(4,128)(2,1)S(1)}, bf16[4,4,4096]{2,0,1:T(4,128)(2,1)S(1)}, u32[]{:S(2)}, u32[]{:S(2)}) collective-permute-start(bf16[4,4,4096]{2,0,1:T(4,128)(2,1)S(1)} %copy.82), channel_id=1, source_target_pairs={{0,1},{1,2},{2,3},{3,4},{4,5},{5,6},{6,7},{7,8},{8,9},{9,10},{10,1... | collective-permute-start | bytes 393224 | tf_op jit(solution)/shard_map/ppermute | solution.py:20
  13.2 1.9 collective-permute-start.3
  15.2 3.1 %collective-permute-start = (bf16[4,4,4096]{2,1,0:T(4,128)(2,1)}, bf16[4,4,4096]{2,1,0:T(4,128)(2,1)S(1)}, u32[]{:S(2)}, u32[]{:S(2)}) collective-permute-start(bf16[4,4,4096]{2,1,0:T(4,128)(2,1)} %param.12), channel_id=1, source_target_pairs={{0,16},{16,32},{32,48},{48,64},{64,80},{80,96},{96,112},{112,128},... | collective-permute-start | bytes 393224 | tf_op jit(solution)/shard_map/ppermute | solution.py:20
  18.3 1.3 collective-permute-start.1
  19.6 0.8 compare_and_fusion.1
  23.2 6.7 %fusion.63 = (bf16[4,4,3,256,128]{4,3,2,1,0:T(8,128)(2,1)}, bf16[4,4,3,256,128]{4,3,2,1,0:T(8,128)(2,1)}) fusion(bf16[4,4,6,256,128]{4,3,2,1,0:T(8,128)(2,1)} %param.11), kind=kLoop, calls=%fused_computation.53 | loop fusion | bytes 12582912 | tf_op jit(solution)/shard_map/slice | solution.py:62
  30.0 1.0 reshape.47
  31.3 3.3 %reshape.45 = bf16[4,4,8,64,64]{4,3,2,1,0:T(8,128)(2,1)S(1)} reshape(bf16[4,4,8,4096]{3,2,1,0:T(8,128)(2,1)} %param.13) | data formatting | bytes 2097152 | tf_op jit(solution)/shard_map/reshape | solution.py:93
  35.1 1.0 gather_fusion.1
  36.4 1.8 gather_fusion
  38.2 1.5 fusion.57
  39.7 29.6 %all-gather.2.cloned.1.call-done = bf16[32,512,256]{2,1,0:T(8,128)(2,1)} async-done(((bf16[2,512,256]{2,1,0:T(8,128)(2,1)}), bf16[32,512,256]{2,1,0:T(8,128)(2,1)}) %all-gather.2.cloned.1.call-update) | async-done | bytes 8388624 | tf_op jit(solution)/shard_map/all_gather | solution.py:46
  69.2 12.0 %broadcast_select_fusion = (bf16[4,3,512,256]{3,0,2,1:T(4,128)(2,1)}, bf16[4,3,512,256]{3,0,2,1:T(4,128)(2,1)}) fusion(pred[]{:T(512)S(6)} %eq.19, bf16[32,512,256]{2,1,0:T(8,128)(2,1)} %all-gather.2.cloned.1.call-done, s32[4,3]{0,1:T(4,128)S(1)} %dynamic-slice_subtract_fusion), kind=kOutput, calls=%fused_computation.19 | convolution fusion | flops 103809408 | bytes 14680113 | tf_op jit(solution)/shard_map/ism,map->isap/dot_general | solution.py:49
  81.2 2.0 pad_maximum_fusion
  83.2 3.3 %reshape.44 = bf16[4,4,8,64,64]{4,3,2,1,0:T(8,128)(2,1)} reshape(bf16[4,4,8,4096]{3,2,1,0:T(8,128)(2,1)S(1)} %pad_maximum_fusion) | data formatting | bytes 2097152 | tf_op jit(solution)/shard_map/reshape | solution.py:90
  86.5 5.3 %fusion.18 = bf16[4,4,8,64,64]{4,3,2,1,0:T(8,128)(2,1)} fusion(bf16[4,4,8,64,64]{4,3,2,1,0:T(8,128)(2,1)S(1)} %reshape.45, bf16[4,4,8,64,64]{4,3,2,1,0:T(8,128)(2,1)} %reshape.44), kind=kOutput, calls=%fused_computation.21 | convolution fusion | flops 134742016 | bytes 3145728 | tf_op jit(solution)/shard_map/ijnac,ijndc->ijnad/dot_general | solution.py:97
  91.8 3.8 %fusion.3 = f32[4,4,1,64,64]{4,2,3,1,0:T(1,128)} fusion(f32[4,4,8,1,1]{2,3,4,1,0:T(1,128)S(1)} %bitcast.64, bf16[4,4,8,64,64]{4,3,2,1,0:T(8,128)(2,1)} %fusion.18), kind=kOutput, calls=%fused_computation.7 | convolution fusion | flops 1048576 | bytes 1311232 | tf_op jit(solution)/shard_map/ijn,ijnad->ijad/dot_general | solution.py:109
  95.6 4.8 %convert_bitcast_fusion.1 = bf16[4,4,3,512,128]{3,4,1,2,0:T(8,128)(2,1)S(1)} fusion(bf16[4,4,3,256,128]{4,3,2,1,0:T(8,128)(2,1)} %get-tuple-element.12, bf16[4,3,512,256,1]{3,0,2,1,4:T(4,128)(2,1)} %bitcast.60), kind=kOutput, calls=%fused_computation.6 | convolution fusion | flops 1613758464 | bytes 12582912 | tf_op jit(solution)/shard_map/isap,ijspq->ijsaq/dot_general | solution.py:53
  101.2 1.7 fusion.22
  103.0 82.1 %all-reduce.2.cloned.1.call-done = bf16[4,3,512,256]{3,0,2,1:T(4,128)(2,1)} async-done(((bf16[4,3,512,256]{3,0,2,1:T(4,128)(2,1)}), bf16[4,3,512,256]{3,0,2,1:T(4,128)(2,1)}) %all-reduce.2.cloned.1.call-update) | async-done | bytes 3145744 | tf_op jit(solution)/shard_map/psum | solution.py:14
  185.1 3.7 %convert_bitcast_fusion = bf16[4,4,3,512,128]{3,4,0,2,1:T(8,128)(2,1)S(1)} fusion(bf16[4,4,3,256,128]{4,3,2,1,0:T(8,128)(2,1)S(1)} %copy-done, bf16[4,3,512,256,1]{3,0,2,1,4:T(4,128)(2,1)} %bitcast.59), kind=kOutput, calls=%fused_computation.5 | convolution fusion | flops 1613758464 | bytes 12582912 | tf_op jit(solution)/shard_map/jsap,ijspq->ijsaq/dot_general | solution.py:59
  190.2 1.0 fusion.52
  191.2 0.9 reshape.46
  (43 shorter events, 6.8 us)
Async XLA Ops:
  6.5 62.7 %all-gather.2.cloned.1.call-start = ((), (), s32[]{:S(2)}) async-start(), calls=%async_computation | async-start | bytes 8912896 | tf_op jit(solution)/shard_map/all_gather | solution.py:46
  7.3 177.8 %all-reduce.2.cloned.1.call-start = ((), (), s32[]{:S(2)}) async-start(), calls=%async_computation.1 | async-start | bytes 6291456 | tf_op jit(solution)/shard_map/psum | solution.py:14
  8.3 26.5 %collective-permute-start.2 = (bf16[4,4,4096]{2,0,1:T(4,128)(2,1)S(1)}, bf16[4,4,4096]{2,0,1:T(4,128)(2,1)S(1)}, u32[]{:S(2)}, u32[]{:S(2)}) collective-permute-start(bf16[4,4,4096]{2,0,1:T(4,128)(2,1)S(1)} %copy.82), channel_id=1, source_target_pairs={{0,1},{1,2},{2,3},{3,4},{4,5},{5,6},{6,7},{7,8},{8,9},{9,10},{10,1... | collective-permute-start | bytes 393224 | tf_op jit(solution)/shard_map/ppermute | solution.py:20
  13.2 21.6 %collective-permute-start.3 = (bf16[4,4,4096]{2,0,1:T(4,128)(2,1)S(1)}, bf16[4,4,4096]{2,0,1:T(4,128)(2,1)S(1)}, u32[]{:S(2)}, u32[]{:S(2)}) collective-permute-start(bf16[4,4,4096]{2,0,1:T(4,128)(2,1)S(1)} %copy.82), channel_id=1, source_target_pairs={{1,0},{2,1},{3,2},{4,3},{5,4},{6,5},{7,6},{8,7},{9,8},{10,9},{11,1... | collective-permute-start | bytes 393224 | tf_op jit(solution)/shard_map/ppermute | solution.py:20
  15.2 20.9 %collective-permute-start = (bf16[4,4,4096]{2,1,0:T(4,128)(2,1)}, bf16[4,4,4096]{2,1,0:T(4,128)(2,1)S(1)}, u32[]{:S(2)}, u32[]{:S(2)}) collective-permute-start(bf16[4,4,4096]{2,1,0:T(4,128)(2,1)} %param.12), channel_id=1, source_target_pairs={{0,16},{16,32},{32,48},{48,64},{64,80},{80,96},{96,112},{112,128},... | collective-permute-start | bytes 393224 | tf_op jit(solution)/shard_map/ppermute | solution.py:20
  18.3 17.8 %collective-permute-start.1 = (bf16[4,4,4096]{2,1,0:T(4,128)(2,1)}, bf16[4,4,4096]{2,1,0:T(4,128)(2,1)S(1)}, u32[]{:S(2)}, u32[]{:S(2)}) collective-permute-start(bf16[4,4,4096]{2,1,0:T(4,128)(2,1)} %param.12), channel_id=1, source_target_pairs={{16,0},{32,16},{48,32},{64,48},{80,64},{96,80},{112,96},{128,112},... | collective-permute-start | bytes 393224 | tf_op jit(solution)/shard_map/ppermute | solution.py:20
  23.2 6.8 %copy-start.4 = (f32[64]{0:T(128)S(1)}, f32[64]{0:T(128)}, u32[]{:S(2)}) copy-start(f32[64]{0:T(128)} %param.15) | copy-start | bytes 772
  23.2 6.8 %copy-start.1 = (bf16[4,4,4096]{2,1,0:T(4,128)(2,1)S(1)}, bf16[4,4,4096]{2,1,0:T(4,128)(2,1)}, u32[]{:S(2)}) copy-start(bf16[4,4,4096]{2,1,0:T(4,128)(2,1)} %param.12) | copy-start | bytes 393220
  101.2 83.8 %copy-start = (bf16[4,4,3,256,128]{4,3,2,1,0:T(8,128)(2,1)S(1)}, bf16[4,4,3,256,128]{4,3,2,1,0:T(8,128)(2,1)}, u32[]{:S(2)}) copy-start(bf16[4,4,3,256,128]{4,3,2,1,0:T(8,128)(2,1)} %get-tuple-element.11) | copy-start | bytes 9437188
  188.8 1.0 copy-start.2
  188.8 1.2 copy-start.3
  188.8 1.2 copy-start.5
  188.8 1.3 copy-start.6
Sparse Core Ops, SparseCore 0:
  9.2 60.0 all-gather.1
  81.4 103.6 all-reduce.1
where the time goes:
time: 199 us
  waiting for transfers between devices  112 us (56%)
  matrix products  32.4 us (16%)
  local copies, waits for them, and re-layouts  22.8 us (11%)
  between operations  13.6 us (7%)
  starting transfers between devices  11.3 us (6%)
  other arithmetic  6.46 us (3%)
    psum x1, waiting for transfers between devices, from_root(): return lax.psum(kept, axis)  82.1 us
    all_gather x1, waiting for transfers between devices, on_device(): piece = lax.all_gather(fitting, 'col', axis=0, tiled=True)  29.6 us
    dot_general x1, matrix products, on_device(): jnp.einsum('ism,map->isap', picker, piece, preferred_element_type=jnp.flo...  12 us
    ppermute x4, starting transfers between devices, passed_along(): return lax.ppermute(block, axis, route)  11.3 us
    slice x1, local copies, waits for them, and re-layouts, on_device(): coefficients[:, :, domain_size:]  6.75 us
    dot_general x1, matrix products, on_device(): jnp.einsum('ijnac,ijndc->ijnad', half, intersection_mats, preferred_eleme...  5.3 us
    dot_general x1, matrix products, on_device(): jnp.einsum('isap,ijspq->ijsaq', row_fit, coefficients[:, :, :domain_size]...  4.82 us
  transfers between devices with their start and end apart: 6, of which 2 were waited for; matrix products, arithmetic and copies ran while one was open for 21% of the time, Pallas kernels for 0%

commit v1 on v0

--- a/solution.py
+++ b/solution.py
@@ -1,23 +1,362 @@
 import jax
 import jax.numpy as jnp
 from jax import lax
+from jax.experimental import pallas as pl
+from jax.experimental.pallas import tpu as pltpu
 from jax.sharding import PartitionSpec as P
 
 AUX = 512
+PAO = 256
 NPNO = 64
 DOMAIN = 3
 PARTNERS = 4
-
-
-def from_root(value, axis, source):
-    kept = jnp.where(lax.axis_index(axis) == source, value, 0).astype(value.dtype)
-    return lax.psum(kept, axis)
+HALF = PAO // 2
+MESH = pl.DeviceIdType.MESH
+F32 = jnp.float32
+BF16 = jnp.bfloat16
 
 
 def passed_along(block, axis, distance):
     devices = range(lax.axis_size(axis))
     route = [(i - distance, i) for i in devices if i - distance in devices]
     return lax.ppermute(block, axis, route)
+
+
+def remote(src, dst, send_sem, recv_sem, row, col):
+    return pltpu.make_async_remote_copy(
+        src_ref=src,
+        dst_ref=dst,
+        send_sem=send_sem,
+        recv_sem=recv_sem,
+        device_id={"row": row, "col": col},
+        device_id_type=MESH,
+    )
+
+
+def arrived(ref, sem):
+    pltpu.make_async_copy(ref, ref, sem).wait()
+
+
+def each(count, body):
+    def step(index, carry):
+        body(index)
+        return carry
+
+    lax.fori_loop(0, count, step, 0)
+
+
+def exchange(
+    rows,
+    cols,
+    i_dev,
+    j_dev,
+    per_dev,
+    orbital_atoms,
+    fitting,
+    coefficients,
+    k_ref,
+    coef,
+    coef_left,
+    total,
+    metric,
+    send_one,
+    row_one,
+    col_one,
+    col_pick,
+    row_all,
+    col_all,
+    coef_sem,
+    send_row_sem,
+    recv_row_sem,
+    send_col_sem,
+    recv_col_sem,
+    gather_row_sem,
+    gathered_row_sem,
+    share_sem,
+    gather_col_sem,
+    gathered_col_sem,
+):
+    row = lax.axis_index("row")
+    col = lax.axis_index("col")
+    core = lax.rem(col, 2)
+    sibling = col + 1 - 2 * core
+    row_atoms = cols * per_dev
+
+    barrier = pltpu.get_barrier_semaphore()
+
+    def signal(row_id, col_id):
+        pl.semaphore_signal(
+            barrier, inc=1, device_id={"row": row_id, "col": col_id}, device_id_type=MESH
+        )
+
+    def greet(other):
+        @pl.when(other != col)
+        def _():
+            signal(row, other)
+
+        @pl.when(other != row)
+        def _():
+            signal(other, col)
+
+        @pl.when((col != row) | (other != col))
+        def _():
+            signal(col, other)
+
+    each(cols, greet)
+
+    for i in range(i_dev):
+        pltpu.make_async_copy(coefficients.at[i], coef.at[i], coef_sem.at[i]).start()
+
+    above = lax.broadcasted_iota(jnp.int32, (HALF, HALF), 0)
+    across = lax.broadcasted_iota(jnp.int32, (HALF, HALF), 1)
+    lower = above > across
+    upper = above < across
+    on = above == across
+    tile_row = lax.broadcasted_iota(jnp.int32, (16, HALF), 0)
+    diagonal = jnp.zeros((16, HALF), F32)
+    for a in range(per_dev):
+        block = fitting[a]
+        square = lax.dot_general(
+            block, block, (((0,), (0,)), ((), ())), preferred_element_type=F32
+        )
+        first = square[:HALF, :HALF]
+        last = square[HALF:, HALF:]
+        triangles = jnp.where(lower, first, jnp.where(upper, last, 0.0)).astype(BF16)
+        cross = square[:HALF, HALF:].astype(BF16)
+        for d in range(cols // 2):
+            send_one[d, a] = triangles[16 * d : 16 * d + 16]
+            send_one[cols // 2 + d, a] = cross[16 * d : 16 * d + 16]
+        for part, piece in ((0, first), (1, last)):
+            line = jnp.sum(jnp.where(on, piece, 0.0), axis=0, keepdims=True)
+            diagonal = jnp.where(tile_row == 2 * a + part, line, diagonal)
+    for d in range(cols):
+        send_one[d, per_dev] = diagonal.astype(BF16)
+
+    pl.semaphore_wait(
+        barrier, cols - 1 + rows - 1 + cols - jnp.where(row == col, 1, 0)
+    )
+
+    def first_row(d):
+        return remote(
+            send_one.at[d], row_one.at[col], send_row_sem.at[d], recv_row_sem.at[col], row, d
+        )
+
+    def first_col(d):
+        return remote(
+            send_one.at[d], col_one.at[col], send_col_sem.at[d], recv_col_sem.at[col], d, row
+        )
+
+    def own_row():
+        return pltpu.make_async_copy(send_one.at[col], row_one.at[col], recv_row_sem.at[col])
+
+    def own_col():
+        return pltpu.make_async_copy(send_one.at[row], col_one.at[col], recv_col_sem.at[col])
+
+    def start_first(step):
+        to_col = lax.rem(row + step, rows)
+
+        @pl.when((col != row) | (to_col != row))
+        def _():
+            first_col(to_col).start()
+
+        to_row = lax.rem(col + step, cols)
+
+        @pl.when(to_row != col)
+        def _():
+            first_row(to_row).start()
+
+    each(cols, start_first)
+    own_row().start()
+
+    @pl.when(row == col)
+    def _():
+        own_col().start()
+
+    for i in range(i_dev):
+        pltpu.make_async_copy(coefficients.at[i], coef.at[i], coef_sem.at[i]).wait()
+
+    def turn(index):
+        i = lax.div(index, j_dev)
+        j = lax.rem(index, j_dev)
+        for s in range(2 * DOMAIN):
+            coef_left[i, j, s] = jnp.transpose(coef[i, j, s])[:NPNO]
+        total[index] = jnp.zeros((NPNO, 2 * NPNO), F32)
+
+    each(i_dev * j_dev, turn)
+
+    each(cols, lambda source: arrived(col_one.at[source], recv_col_sem.at[source]))
+
+    def wanted(owner, slot):
+        orbital = owner * i_dev + lax.div(slot, DOMAIN)
+        atom = orbital_atoms[orbital, lax.rem(slot, DOMAIN)] - owner * row_atoms
+        atom = jnp.clip(atom, 0, row_atoms - 1)
+        return lax.div(atom, per_dev), lax.rem(atom, per_dev)
+
+    def pick_col(slot):
+        source, place = wanted(col, slot)
+        col_pick[slot] = col_one[source, place]
+
+    each(j_dev * DOMAIN, pick_col)
+
+    def gather_col(other):
+        return remote(
+            col_pick, col_all.at[row], gather_col_sem.at[other], gathered_col_sem.at[row], other, col
+        )
+
+    def start_col(step):
+        gather_col(lax.rem(row + 1 + step, rows)).start()
+
+    each(rows - 1, start_col)
+    own = pltpu.make_async_copy(col_pick, col_all.at[row], gathered_col_sem.at[row])
+    own.start()
+
+    each(cols, lambda source: arrived(row_one.at[source], recv_row_sem.at[source]))
+
+    def pick_row(slot):
+        source, place = wanted(row, slot)
+        row_all[col, slot] = row_one[source, place]
+
+    each(i_dev * DOMAIN, pick_row)
+
+    def gather_row(other):
+        return remote(
+            row_all.at[col], row_all.at[col], gather_row_sem.at[other], gathered_row_sem.at[col], row, other
+        )
+
+    def share_row(source):
+        return remote(
+            row_all.at[source], row_all.at[source], share_sem.at[source], gathered_row_sem.at[source], row, sibling
+        )
+
+    gather_row(sibling).start()
+
+    def peer(step):
+        return lax.rem(col + 2 * (step + 1), cols)
+
+    each(cols // 2 - 1, lambda step: gather_row(peer(step)).start())
+
+    def share(step):
+        source = peer(step)
+        arrived(row_all.at[source], gathered_row_sem.at[source])
+        share_row(source).start()
+
+    each(cols // 2 - 1, share)
+
+    def from_sibling(step):
+        source = lax.rem(sibling + 2 * step, cols)
+        arrived(row_all.at[source], gathered_row_sem.at[source])
+
+    each(cols // 2, from_sibling)
+
+    def build(held, one, owner, slot):
+        packed = held[:, slot].reshape(PAO, HALF)
+        source, place = wanted(owner, slot)
+        lines = one[source, per_dev].astype(F32)
+        first_line = jnp.where(place == 0, lines[0:1], lines[2:3])
+        last_line = jnp.where(place == 0, lines[1:2], lines[3:4])
+        triangles = packed[:HALF].astype(F32)
+        turned = jnp.transpose(triangles)
+        cross = packed[HALF:].astype(F32)
+        first = jnp.where(lower, triangles, jnp.where(upper, turned, first_line))
+        last = jnp.where(upper, triangles, jnp.where(lower, turned, last_line))
+        metric[:HALF, :HALF] = first.astype(BF16)
+        metric[:HALF, HALF:] = cross.astype(BF16)
+        metric[HALF:, :HALF] = jnp.transpose(cross).astype(BF16)
+        metric[HALF:, HALF:] = last.astype(BF16)
+
+    def apply(i, j, s):
+        mapped = jnp.dot(metric[...], coef[i, j, s], preferred_element_type=F32).astype(BF16)
+        total[i * j_dev + j] += jnp.dot(
+            coef_left[i, j, s], mapped, preferred_element_type=F32
+        )
+
+    def row_slot(slot):
+        build(row_all, row_one, row, slot)
+        for j in range(j_dev):
+            apply(lax.div(slot, DOMAIN), j, lax.rem(slot, DOMAIN))
+
+    each(i_dev * DOMAIN, row_slot)
+
+    each(rows, lambda source: arrived(col_all.at[source], gathered_col_sem.at[source]))
+
+    def col_slot(slot):
+        build(col_all, col_one, col, slot)
+        for i in range(i_dev):
+            apply(i, lax.div(slot, DOMAIN), DOMAIN + lax.rem(slot, DOMAIN))
+
+    each(j_dev * DOMAIN, col_slot)
+
+    k_ref[...] = total[...]
+
+    def finish_first(step):
+        to_col = lax.rem(row + step, rows)
+
+        @pl.when((col != row) | (to_col != row))
+        def _():
+            first_col(to_col).wait_send()
+
+        to_row = lax.rem(col + step, cols)
+
+        @pl.when(to_row != col)
+        def _():
+            first_row(to_row).wait_send()
+
+    each(cols, finish_first)
+    each(rows - 1, lambda step: gather_col(lax.rem(row + 1 + step, rows)).wait_send())
+    gather_row(sibling).wait_send()
+    each(cols // 2 - 1, lambda step: gather_row(peer(step)).wait_send())
+    each(cols // 2 - 1, lambda step: share_row(peer(step)).wait_send())
+
+
+def exchange_part_of(fitting, coefficients, orbital_atoms):
+    rows = lax.axis_size("row")
+    cols = lax.axis_size("col")
+    i_dev, j_dev = coefficients.shape[:2]
+    per_dev = fitting.shape[0]
+    slots = i_dev * DOMAIN
+
+    def body(*refs):
+        exchange(rows, cols, i_dev, j_dev, per_dev, *refs)
+
+    dma = pltpu.SemaphoreType.DMA
+    slices = (per_dev + 1, 16, HALF)
+    out = pl.pallas_call(
+        body,
+        out_shape=jax.ShapeDtypeStruct((i_dev * j_dev, NPNO, 2 * NPNO), F32),
+        in_specs=[
+            pl.BlockSpec(memory_space=pltpu.SMEM),
+            pl.BlockSpec(memory_space=pltpu.VMEM),
+            pl.BlockSpec(memory_space=pl.ANY),
+        ],
+        out_specs=pl.BlockSpec(memory_space=pltpu.VMEM),
+        scratch_shapes=[
+            pltpu.VMEM(coefficients.shape, BF16),
+            pltpu.VMEM((i_dev, j_dev, 2 * DOMAIN, NPNO, PAO), BF16),
+            pltpu.VMEM((i_dev * j_dev, NPNO, 2 * NPNO), F32),
+            pltpu.VMEM((PAO, PAO), BF16),
+            pltpu.VMEM((cols,) + slices, BF16),
+            pltpu.VMEM((cols,) + slices, BF16),
+            pltpu.VMEM((cols,) + slices, BF16),
+            pltpu.VMEM((slots, 16, HALF), BF16),
+            pltpu.VMEM((cols, slots, 16, HALF), BF16),
+            pltpu.VMEM((rows, slots, 16, HALF), BF16),
+            dma((i_dev,)),
+            dma((cols,)),
+            dma((cols,)),
+            dma((rows,)),
+            dma((cols,)),
+            dma((cols,)),
+            dma((cols,)),
+            dma((cols,)),
+            dma((rows,)),
+            dma((rows,)),
+        ],
+        compiler_params=pltpu.CompilerParams(
+            collective_id=0, has_side_effects=True, vmem_limit_bytes=48 * 1024 * 1024
+        ),
+        name="exchange",
+    )(orbital_atoms, fitting, coefficients)
+    return out.reshape(i_dev, j_dev, NPNO, 2 * NPNO)[..., NPNO:]
 
 
 def on_device(
@@ -34,46 +373,11 @@
 ):
     row_count = amplitudes.shape[0]
     column_count = amplitudes.shape[1]
-    domain_size = orbital_atoms.shape[1]
     row_place = lax.axis_index("row")
     column_place = lax.axis_index("col")
-    row_atoms = fitting.shape[0] * lax.axis_size("col")
     first_row = row_place * row_count
     first_column = column_place * column_count
-    wanted = (
-        lax.dynamic_slice_in_dim(orbital_atoms, first_row, row_count, 0) - row_place * row_atoms
-    )
-    piece = lax.all_gather(fitting, "col", axis=0, tiled=True)
-    labels = jnp.arange(piece.shape[0], dtype=jnp.int32)
-    picker = (wanted[:, :, None] == labels[None, None, :]).astype(jnp.bfloat16)
-    added = jnp.einsum("ism,map->isap", picker, piece, preferred_element_type=jnp.float32)
-    row_fit = added.astype(jnp.bfloat16)
-    source_row = first_column // row_count
-    column_fit = from_root(row_fit, "row", source_row)
-    own_side = jnp.einsum(
-        "isap,ijspq->ijsaq",
-        row_fit,
-        coefficients[:, :, :domain_size],
-        preferred_element_type=jnp.float32,
-    ).astype(jnp.bfloat16)
-    other_side = jnp.einsum(
-        "jsap,ijspq->ijsaq",
-        column_fit,
-        coefficients[:, :, domain_size:],
-        preferred_element_type=jnp.float32,
-    ).astype(jnp.bfloat16)
-    exchange_part = jnp.einsum(
-        "ijsaq,ijsar->ijqr",
-        own_side[..., :NPNO],
-        own_side[..., NPNO:],
-        preferred_element_type=jnp.float32,
-    )
-    exchange_part = exchange_part + jnp.einsum(
-        "ijsaq,ijsar->ijqr",
-        other_side[..., :NPNO],
-        other_side[..., NPNO:],
-        preferred_element_type=jnp.float32,
-    )
+    exchange_part = exchange_part_of(fitting, coefficients, orbital_atoms)
     exchange_part = exchange_part * (2 * DOMAIN * AUX) ** (-0.5)
     row_partner = lax.dynamic_slice_in_dim(fock_partner, first_row, row_count, 0)
     column_partner = lax.dynamic_slice_in_dim(fock_partner, first_column, column_count, 0)

time: 199 us -> 127 us (0.64); the launches traced: 199 us -> 125 us
  waiting for transfers between devices: 112 us -> 0.01 us
  Pallas kernels: 0 us -> 76.1 us
  matrix products: 32.4 us -> 8.32 us
  between operations: 13.6 us -> 0.13 us
  local copies, waits for them, and re-layouts: 22.8 us -> 17.5 us
  other arithmetic: 6.46 us -> 11.3 us
    psum x1 -> x0, waiting for transfers between devices: 82.1 us -> none  [from_root(): return lax.psum(kept, axis)]
    pallas_call x0 -> x1, Pallas kernels: none -> 76.1 us  [exchange_part_of(): pl.pallas_call(body, out_shape=jax.ShapeDtypeStruct((i_dev * j_dev, NPNO,...]
    all_gather x1 -> x0, waiting for transfers between devices: 29.6 us -> none  [on_device(): piece = lax.all_gather(fitting, 'col', axis=0, tiled=True)]
    dot_general x5 -> x0, matrix products: 23.3 us -> none  [the longest x1 12 us: on_device(): jnp.einsum('ism,map->isap', picker, piece, preferred_element_type=jnp.flo...]
    slice x3 -> x0, local copies, waits for them, and re-layouts: 7.99 us -> none  [the longest x1 6.75 us: on_device(): coefficients[:, :, domain_size:]]
    select_n x0 -> x2, other arithmetic: none -> 2.25 us  [the longest x1 1.76 us: on_device(): jnp.take(row_source, row_pick, axis=0)]
  transfers between devices with their start and end apart: 6 -> 4, of which waited for: 2 -> 0; matrix products, arithmetic and copies ran while one was open for 21% -> 12% of each run, Pallas kernels for 0% -> 61%
where the time goes in v1:
time: 127 us; the launch traced here: 125 us
  Pallas kernels  76.1 us (60%)
  local copies, waits for them, and re-layouts  17.5 us (14%)
  starting transfers between devices  11.3 us (9%)
  other arithmetic  11.3 us (9%)
  matrix products  8.32 us (7%)
    pallas_call x1, Pallas kernels, exchange_part_of(): pl.pallas_call(body, out_shape=jax.ShapeDtypeStruct((i_dev * j_dev, NPNO,...  76.1 us
    ppermute x4, starting transfers between devices, passed_along(): return lax.ppermute(block, axis, route)  11.3 us
    dot_general x1, matrix products, on_device(): jnp.einsum('ijnac,ijndc->ijnad', half, intersection_mats, preferred_eleme...  5.26 us
    reshape x1, local copies, waits for them, and re-layouts, on_device(): jnp.concatenate([from_rows, from_columns], axis=2)  4.36 us
    reshape x1, local copies, waits for them, and re-layouts, on_device(): intersections.reshape(row_count, column_count, 2 * PARTNERS, NPNO, NPNO)  3.25 us
    dot_general x1, matrix products, on_device(): coupling = jnp.einsum('ijn,ijnad->ijad', weights, sandwich)  3.06 us
    concatenate x1, other arithmetic, on_device(): jnp.concatenate([from_rows, from_columns], axis=2)  2.71 us
  transfers between devices with their start and end apart: 4, of which 0 were waited for; matrix products, arithmetic and copies ran while one was open for 12% of the time, Pallas kernels for 61%

profile of v1, /device:TPU:1, one launch (start us, length us, event | category | flops | bytes accessed | tf_op | source)
XLA Modules:
  0.0 124.6 jit_solution(6213484804092094344)
XLA Ops:
  0.0 1.1 copy.26
  1.1 4.9 %collective-permute-start.2 = (bf16[4,4,4096]{2,0,1:T(4,128)(2,1)S(1)}, bf16[4,4,4096]{2,0,1:T(4,128)(2,1)}, u32[]{:S(2)}, u32[]{:S(2)}) collective-permute-start(bf16[4,4,4096]{2,0,1:T(4,128)(2,1)S(1)} %copy.26), channel_id=1, source_target_pairs={{0,1},{1,2},{2,3},{3,4},{4,5},{5,6},{6,7},{7,8},{8,9},{9,10},{10,1... | collective-permute-start | bytes 393224 | tf_op jit(solution)/shard_map/ppermute | solution.py:22
  6.0 2.1 %collective-permute-start.3 = (bf16[4,4,4096]{2,0,1:T(4,128)(2,1)S(1)}, bf16[4,4,4096]{2,0,1:T(4,128)(2,1)}, u32[]{:S(2)}, u32[]{:S(2)}) collective-permute-start(bf16[4,4,4096]{2,0,1:T(4,128)(2,1)S(1)} %copy.26), channel_id=1, source_target_pairs={{1,0},{2,1},{3,2},{4,3},{5,4},{6,5},{7,6},{8,7},{9,8},{10,9},{11,1... | collective-permute-start | bytes 393224 | tf_op jit(solution)/shard_map/ppermute | solution.py:22
  8.1 2.9 %collective-permute-start = (bf16[4,4,4096]{2,1,0:T(4,128)(2,1)}, bf16[4,4,4096]{2,1,0:T(4,128)(2,1)S(1)}, u32[]{:S(2)}, u32[]{:S(2)}) collective-permute-start(bf16[4,4,4096]{2,1,0:T(4,128)(2,1)} %param.12), channel_id=1, source_target_pairs={{0,16},{16,32},{32,48},{48,64},{64,80},{80,96},{96,112},{112,128},... | collective-permute-start | bytes 393224 | tf_op jit(solution)/shard_map/ppermute | solution.py:22
  11.1 1.3 %collective-permute-start.1 = (bf16[4,4,4096]{2,1,0:T(4,128)(2,1)}, bf16[4,4,4096]{2,1,0:T(4,128)(2,1)}, u32[]{:S(2)}, u32[]{:S(2)}) collective-permute-start(bf16[4,4,4096]{2,1,0:T(4,128)(2,1)} %param.12), channel_id=1, source_target_pairs={{16,0},{32,16},{48,32},{64,48},{80,64},{96,80},{112,96},{128,112},... | collective-permute-start | bytes 393224 | tf_op jit(solution)/shard_map/ppermute | solution.py:22
  12.4 0.8 compare_and_fusion.1
  13.6 0.8 constant_dynamic-slice_fusion.1
  14.4 0.8 iota_compare_fusion
  15.2 0.8 fusion.14
  16.0 1.9 %reshape.50 = f32[4,4,64,64]{3,2,1,0:T(8,128)} reshape(bf16[4,4,4096]{2,1,0:T(4,128)(2,1)} %param.12) | data formatting | bytes 393216 | tf_op jit(solution)/shard_map/convert_element_type | solution.py:422
  18.0 3.3 %reshape.48 = bf16[4,4,8,64,64]{4,3,2,1,0:T(8,128)(2,1)S(1)} reshape(bf16[4,4,8,4096]{3,2,1,0:T(8,128)(2,1)} %param.13) | data formatting | bytes 2097152 | tf_op jit(solution)/shard_map/reshape | solution.py:397
  21.6 76.1 %exchange.1 = f32[16,64,128]{2,1,0:T(8,128)S(1)} custom-call(s32[64,3]{1,0:T(8,128)S(1)} %copy.20.refs_0_, bf16[2,512,256]{2,1,0:T(8,128)(2,1)S(1)} %copy-done, bf16[4,4,6,256,128]{4,3,2,1,0:T(8,128)(2,1)} %refs_2_.1), custom_call_target="tpu_custom_call" | custom-call | tf_op jit(solution)/shard_map/exchange/pallas_call | solution.py:323
  97.8 1.2 %pad_maximum_fusion.2 = bf16[4,12,4096]{2,0,1:T(4,128)(2,1)S(1)} fusion(bf16[4,4,4096]{2,0,1:T(4,128)(2,1)} %collective-permute-done.3, bf16[4,4,4096]{2,0,1:T(4,128)(2,1)S(1)} %copy.26, bf16[4,4,4096]{2,0,1:T(4,128)(2,1)} %collective-permute-done.2), kind=kLoop, calls=%fused_computation.17 | loop fusion | flops 393216 | bytes 786432 | tf_op jit(solution)/shard_map/concatenate | solution.py:389
  99.1 1.8 %gather_fusion.1 = bf16[16,4,4096]{2,1,0:T(4,128)(2,1)} fusion(bf16[4,12,4096]{2,0,1:T(4,128)(2,1)S(1)} %pad_maximum_fusion.2, s32[1024]{0:T(1024)S(1)} %pad_clamp_fusion), kind=kCustom, calls=%fused_computation.1 | custom fusion | bytes 1048640 | tf_op jit(solution)/shard_map/jit(_take)/gather | solution.py:393
  100.8 2.2 %select_bitcast_fusion = bf16[4,4,4,4096]{3,0,2,1:T(4,128)(2,1)} fusion(bf16[4,4,4,4096]{3,2,1,0:T(4,128)(2,1)} %bitcast.24, pred[4,4]{1,0:T(4,128)(4,1)S(1)} %copy.25), kind=kLoop, calls=%fused_computation.15 | loop fusion | flops 262144 | bytes 1048592 | tf_op jit(solution)/shard_map/jit(_take)/select_n | solution.py:393
  103.0 1.2 pad_maximum_fusion.1
  104.2 1.8 %gather_fusion = bf16[16,4,4096]{2,1,0:T(4,128)(2,1)} fusion(bf16[12,4,4096]{2,1,0:T(4,128)(2,1)S(1)} %pad_maximum_fusion.1, s32[1024]{0:T(1024)S(1)} %pad_clamp_fusion.1), kind=kCustom, calls=%fused_computation | custom fusion | bytes 1048640 | tf_op jit(solution)/shard_map/jit(_take)/gather | solution.py:392
  106.0 1.8 %fusion.13 = bf16[4,4,4,4096]{3,0,2,1:T(4,128)(2,1)S(1)} fusion(bf16[4,4,4,4096]{3,2,1,0:T(4,128)(2,1)} %bitcast.23, pred[4,4]{0,1:T(4,128)(4,1)S(1)} %get-tuple-element.5), kind=kLoop, calls=%fused_computation.14 | loop fusion | flops 262144 | bytes 1048592 | tf_op jit(solution)/shard_map/jit(_take)/select_n | solution.py:392
  107.7 2.7 %pad_maximum_fusion = bf16[4,4,8,4096]{3,0,2,1:T(4,128)(2,1)} fusion(bf16[4,4,4,4096]{3,0,2,1:T(4,128)(2,1)} %select_bitcast_fusion, bf16[4,4,4,4096]{3,0,2,1:T(4,128)(2,1)S(1)} %fusion.13), kind=kLoop, calls=%fused_computation.8 | loop fusion | flops 524288 | bytes 2097152 | tf_op jit(solution)/shard_map/concatenate | solution.py:394
  110.4 4.4 %reshape.47 = bf16[4,4,8,64,64]{4,3,0,2,1:T(8,128)(2,1)} reshape(bf16[4,4,8,4096]{3,0,2,1:T(4,128)(2,1)} %pad_maximum_fusion) | data formatting | bytes 2097152 | tf_op jit(solution)/shard_map/reshape | solution.py:394
  114.8 5.3 %fusion.4 = bf16[4,4,8,64,64]{4,3,2,1,0:T(8,128)(2,1)} fusion(bf16[4,4,8,64,64]{4,3,2,1,0:T(8,128)(2,1)S(1)} %reshape.48, bf16[4,4,8,64,64]{4,3,0,2,1:T(8,128)(2,1)} %reshape.47), kind=kOutput, calls=%fused_computation.6 | convolution fusion | flops 134742016 | bytes 3145728 | tf_op jit(solution)/shard_map/ijnac,ijndc->ijnad/dot_general | solution.py:401
  120.1 3.1 %fusion = f32[4,4,1,64,64]{4,2,3,1,0:T(1,128)S(1)} fusion(f32[4,4,8,1,1]{2,3,4,1,0:T(1,128)S(1)} %bitcast.25, bf16[4,4,8,64,64]{4,3,2,1,0:T(8,128)(2,1)} %fusion.4), kind=kOutput, calls=%fused_computation.2 | convolution fusion | flops 1048576 | bytes 1311232 | tf_op jit(solution)/shard_map/ijn,ijnad->ijad/dot_general | solution.py:413
  123.1 0.5 fusion.12
  123.6 0.9 reshape.49
  (27 shorter events, 0.9 us)
Async XLA Ops:
  0.0 21.5 %copy-start.4 = (s32[64,3]{0,1:T(4,128)S(1)}, s32[64,3]{0,1:T(4,128)}, u32[]{:S(2)}) copy-start(s32[64,3]{0,1:T(4,128)} %param.17) | copy-start | bytes 2308
  0.0 21.6 %copy-start = (bf16[2,512,256]{2,1,0:T(8,128)(2,1)S(1)}, bf16[2,512,256]{2,1,0:T(8,128)(2,1)}, u32[]{:S(2)}) copy-start(bf16[2,512,256]{2,1,0:T(8,128)(2,1)} %refs_1_.1) | copy-start | bytes 1572868
  1.1 96.8 %collective-permute-start.2 = (bf16[4,4,4096]{2,0,1:T(4,128)(2,1)S(1)}, bf16[4,4,4096]{2,0,1:T(4,128)(2,1)}, u32[]{:S(2)}, u32[]{:S(2)}) collective-permute-start(bf16[4,4,4096]{2,0,1:T(4,128)(2,1)S(1)} %copy.26), channel_id=1, source_target_pairs={{0,1},{1,2},{2,3},{3,4},{4,5},{5,6},{6,7},{7,8},{8,9},{9,10},{10,1... | collective-permute-start | bytes 393224 | tf_op jit(solution)/shard_map/ppermute | solution.py:22
  6.0 91.8 %collective-permute-start.3 = (bf16[4,4,4096]{2,0,1:T(4,128)(2,1)S(1)}, bf16[4,4,4096]{2,0,1:T(4,128)(2,1)}, u32[]{:S(2)}, u32[]{:S(2)}) collective-permute-start(bf16[4,4,4096]{2,0,1:T(4,128)(2,1)S(1)} %copy.26), channel_id=1, source_target_pairs={{1,0},{2,1},{3,2},{4,3},{5,4},{6,5},{7,6},{8,7},{9,8},{10,9},{11,1... | collective-permute-start | bytes 393224 | tf_op jit(solution)/shard_map/ppermute | solution.py:22
  8.1 94.9 %collective-permute-start = (bf16[4,4,4096]{2,1,0:T(4,128)(2,1)}, bf16[4,4,4096]{2,1,0:T(4,128)(2,1)S(1)}, u32[]{:S(2)}, u32[]{:S(2)}) collective-permute-start(bf16[4,4,4096]{2,1,0:T(4,128)(2,1)} %param.12), channel_id=1, source_target_pairs={{0,16},{16,32},{32,48},{48,64},{64,80},{80,96},{96,112},{112,128},... | collective-permute-start | bytes 393224 | tf_op jit(solution)/shard_map/ppermute | solution.py:22
  11.1 91.9 %collective-permute-start.1 = (bf16[4,4,4096]{2,1,0:T(4,128)(2,1)}, bf16[4,4,4096]{2,1,0:T(4,128)(2,1)}, u32[]{:S(2)}, u32[]{:S(2)}) collective-permute-start(bf16[4,4,4096]{2,1,0:T(4,128)(2,1)} %param.12), channel_id=1, source_target_pairs={{16,0},{32,16},{48,32},{64,48},{80,64},{96,80},{112,96},{128,112},... | collective-permute-start | bytes 393224 | tf_op jit(solution)/shard_map/ppermute | solution.py:22
  97.7 5.3 %copy-start.2 = (bf16[4,4,4096]{2,1,0:T(4,128)(2,1)S(1)}, bf16[4,4,4096]{2,1,0:T(4,128)(2,1)}, u32[]{:S(2)}) copy-start(bf16[4,4,4096]{2,1,0:T(4,128)(2,1)} %param.12) | copy-start | bytes 393220
  120.1 3.1 %copy-start.1 = (f32[4,4,64,64]{3,2,1,0:T(8,128)S(1)}, f32[4,4,64,64]{3,2,1,0:T(8,128)}, u32[]{:S(2)}) copy-start(f32[4,4,64,64]{3,2,1,0:T(8,128)} %reshape.50) | copy-start | bytes 786436
  120.1 3.1 %copy-start.3 = (f32[4,4,64]{2,1,0:T(4,128)S(1)}, f32[4,4,64]{2,1,0:T(4,128)}, u32[]{:S(2)}) copy-start(f32[4,4,64]{2,1,0:T(4,128)} %param.14) | copy-start | bytes 12292

commit v2 on v1

v2 whole, which is shorter than its diff:
```python
import jax
import jax.numpy as jnp
from jax import lax
from jax.experimental import pallas as pl
from jax.experimental.pallas import tpu as pltpu
from jax.sharding import PartitionSpec as P

AUX = 512
PAO = 256
NPNO = 64
DOMAIN = 3
PARTNERS = 4
HALF = PAO // 2
MESH = pl.DeviceIdType.MESH
SKIP = frozenset()
F32 = jnp.float32
BF16 = jnp.bfloat16


SUB = 8
LANES = 128
PAIR = 2 * NPNO
CHUNKS = NPNO * NPNO // LANES


def remote(src, dst, send_sem, recv_sem, row, col):
    return pltpu.make_async_remote_copy(
        src_ref=src,
        dst_ref=dst,
        send_sem=send_sem,
        recv_sem=recv_sem,
        device_id={"row": row, "col": col},
        device_id_type=MESH,
    )


def arrived(ref, sem):
    pltpu.make_async_copy(ref, ref, sem).wait()


def each(count, body):
    def step(index, carry):
        body(index)
        return carry

    lax.fori_loop(0, count, step, 0)


def swap_halves(value):
    return pltpu.roll(value, NPNO, 1)


def low_lanes(shape):
    return lax.broadcasted_iota(jnp.int32, shape, 1) % LANES < NPNO


def join(first, second):
    low = low_lanes(first.shape)
    left = jnp.where(low, first, swap_halves(second))
    right = jnp.where(low, swap_halves(first), second)
    return left, right


def spread(block, scratch):
    count = block.shape[0]
    for k in range(CHUNKS):
        scratch[SUB * k : SUB * k + count, :] = block[:, LANES * k : LANES * k + LANES].astype(F32)


def packed_of(scratch, n):
    return scratch[pl.ds(n, CHUNKS, stride=SUB), :]


def twice_on_diagonal(packed, scratch):
    scratch[pl.ds(0, CHUNKS, stride=2), :] = packed
    scratch[pl.ds(1, CHUNKS, stride=2), :] = swap_halves(packed)
    rows = scratch[...]
    low = low_lanes(rows.shape)
    upper = jnp.where(low, rows, 0.0)
    lower = jnp.where(low, 0.0, swap_halves(rows))
    return jnp.concatenate([upper, lower], axis=0).astype(BF16)


def split_twice(packed):
    turned = swap_halves(packed)
    low = low_lanes(packed.shape)
    zero = jnp.zeros_like(packed)
    return jnp.concatenate(
        [
            jnp.where(low, packed, zero),
            jnp.where(low, turned, zero),
            jnp.where(low, zero, turned),
            jnp.where(low, zero, packed),
        ],
        axis=0,
    ).astype(BF16)


def residual_kernel(
    rows,
    cols,
    i_dev,
    j_dev,
    per_dev,
    orbital_atoms,
    fock_partner,
    fock_value,
    occupied,
    kept,
    fitting,
    amplitudes,
    energies,
    coefficients,
    intersections,
    out_ref,
    coef,
    inter,
    left_row,
    right_row,
    left_col,
    right_col,
    total_row,
    total_col,
    metric,
    send_one,
    relay,
    row_one,
    col_one,
    col_pick,
    row_all,
    col_all,
    halo,
    source_row,
    source_col,
    current,
    coupled,
    spread_scr,
    rows_scr,
    coef_sem,
    inter_sem,
    send_row_sem,
    recv_row_sem,
    send_relay_sem,
    recv_relay_sem,
    send_col_sem,
    recv_col_sem,
    gather_row_sem,
    gathered_row_sem,
    share_sem,
    gather_col_sem,
    gathered_col_sem,
    send_halo_sem,
    recv_halo_sem,
):
    row = lax.axis_index("row")
    col = lax.axis_index("col")
    core = lax.rem(col, 2)
    sibling = col + 1 - 2 * core
    row_atoms = cols * per_dev
    slots = i_dev * DOMAIN

    barrier = pltpu.get_barrier_semaphore()

    def greet(step):
        other = lax.rem(row + 1 + step, rows)
        pl.semaphore_signal(
            barrier, inc=1, device_id={"row": other, "col": col}, device_id_type=MESH
        )
        other = lax.rem(col + 1 + step, cols)
        pl.semaphore_signal(
            barrier, inc=1, device_id={"row": row, "col": other}, device_id_type=MESH
        )

    each(rows - 1, greet)

    def load_coef(i):
        return pltpu.make_async_copy(coefficients.at[i], coef.at[i], coef_sem.at[i])

    def load_inter(i):
        return pltpu.make_async_copy(intersections.at[i], inter.at[i], inter_sem.at[i])

    for i in range(i_dev):
        load_coef(i).start()
    for i in range(i_dev):
        load_inter(i).start()

    above = lax.broadcasted_iota(jnp.int32, (HALF, HALF), 0)
    across = lax.broadcasted_iota(jnp.int32, (HALF, HALF), 1)
    lower = above > across
    upper = above < across
    on = above == across
    tile_row = lax.broadcasted_iota(jnp.int32, (16, HALF), 0)
    diagonal = jnp.zeros((16, HALF), F32)
    for a in range(per_dev):
        block = fitting[a]
        square = lax.dot_general(
            block, block, (((0,), (0,)), ((), ())), preferred_element_type=F32
        )
        first = square[:HALF, :HALF]
        last = square[HALF:, HALF:]
        triangles = jnp.where(lower, first, jnp.where(upper, last, 0.0)).astype(BF16)
        cross = square[:HALF, HALF:].astype(BF16)
        for d in range(cols // 2):
            send_one[d, a] = triangles[16 * d : 16 * d + 16]
            send_one[cols // 2 + d, a] = cross[16 * d : 16 * d + 16]
        for part, piece in ((0, first), (1, last)):
            line = jnp.sum(jnp.where(on, piece, 0.0), axis=0, keepdims=True)
            diagonal = jnp.where(tile_row == 2 * a + part, line, diagonal)
    for d in range(cols):
        send_one[d, per_dev] = diagonal.astype(BF16)

    pl.semaphore_wait(barrier, cols - 1 + rows - 1)

    def to_plane(other):
        return remote(
            send_one.at[other], relay.at[row], send_relay_sem.at[other], recv_relay_sem.at[row], other, col
        )

    def to_row(other):
        return remote(
            send_one.at[other], row_one.at[col], send_row_sem.at[other], recv_row_sem.at[col], row, other
        )

    def to_col(other):
        return remote(
            relay.at[other], col_one.at[col], send_col_sem.at[other], recv_col_sem.at[col], row, other
        )

    def to_halo(place):
        other_row = lax.rem(row + (rows + 1, rows - 1, rows, rows)[place], rows)
        other_col = lax.rem(col + (cols, cols, cols + 1, cols - 1)[place], cols)
        return remote(
            amplitudes, halo.at[place], send_halo_sem.at[place], recv_halo_sem.at[place], other_row, other_col
        )

    def other_row(step):
        return lax.rem(row + 1 + step, rows)

    def other_col(step):
        return lax.rem(col + 1 + step, cols)

    def start_first(step):
        to_plane(other_row(step)).start()
        to_row(other_col(step)).start()

    each(rows - 1, start_first)
    pltpu.make_async_copy(send_one.at[row], relay.at[row], recv_relay_sem.at[row]).start()
    pltpu.make_async_copy(send_one.at[col], row_one.at[col], recv_row_sem.at[col]).start()
    for place in range(4):
        to_halo(place).start()

    def order_row(slot):
        i, s = lax.div(slot, DOMAIN), lax.rem(slot, DOMAIN)
        lefts, rights = [], []
        for j in range(0, j_dev, 2):
            left, right = join(coef[i, j, s], coef[i, j + 1, s])
            lefts.append(left)
            rights.append(right)
        left_row[slot] = jnp.transpose(jnp.concatenate(lefts, axis=1))
        right_row[slot] = jnp.concatenate(rights, axis=1)

    def order_col(slot):
        j, s = lax.div(slot, DOMAIN), DOMAIN + lax.rem(slot, DOMAIN)
        lefts, rights = [], []
        for i in range(0, i_dev, 2):
            left, right = join(coef[i, j, s], coef[i + 1, j, s])
            lefts.append(left)
            rights.append(right)
        left_col[slot] = jnp.transpose(jnp.concatenate(lefts, axis=1))
        right_col[slot] = jnp.concatenate(rights, axis=1)

    for i in range(i_dev):
        load_coef(i).wait()
    if "turn" not in SKIP:
        each(slots, order_row)

    def pass_on(step):
        other = other_row(step)
        arrived(relay.at[other], recv_relay_sem.at[other])

        @pl.when(other != col)
        def _():
            to_col(other).start()

        @pl.when(other == col)
        def _():
            pltpu.make_async_copy(relay.at[other], col_one.at[col], recv_col_sem.at[col]).start()

    each(rows, pass_on)

    each(cols, lambda source: arrived(row_one.at[source], recv_row_sem.at[source]))

    def wanted(owner, slot):
        orbital = owner * i_dev + lax.div(slot, DOMAIN)
        atom = orbital_atoms[orbital, lax.rem(slot, DOMAIN)] - owner * row_atoms
        atom = jnp.clip(atom, 0, row_atoms - 1)
        return lax.div(atom, per_dev), lax.rem(atom, per_dev)

    def pick_row(slot):
        source, place = wanted(row, slot)
        row_all[col, slot] = row_one[source, place]

    each(slots, pick_row)

    def gather_row(other):
        return remote(
            row_all.at[col], row_all.at[col], gather_row_sem.at[other], gathered_row_sem.at[col], row, other
        )

    def share_row(source):
        return remote(
            row_all.at[source], row_all.at[source], share_sem.at[source], gathered_row_sem.at[source], row, sibling
        )

    def peer(step):
        return lax.rem(col + 2 * (step + 1), cols)

    each(cols // 2 - 1, lambda step: gather_row(peer(step)).start())
    gather_row(sibling).start()

    if "turn" not in SKIP:
        each(slots, order_col)

    each(cols, lambda source: arrived(col_one.at[source], recv_col_sem.at[source]))

    def pick_col(slot):
        source, place = wanted(col, slot)
        col_pick[slot] = col_one[source, place]

    each(slots, pick_col)

    def gather_col(other):
        return remote(
            col_pick, col_all.at[row], gather_col_sem.at[other], gathered_col_sem.at[row], other, col
        )

    each(rows - 1, lambda step: gather_col(other_row(step)).start())
    pltpu.make_async_copy(col_pick, col_all.at[row], gathered_col_sem.at[row]).start()

    for place in range(4):
        arrived(halo.at[place], recv_halo_sem.at[place])

    def sources(place, block, first_row, first_col):
        def step(a):
            spread(block[a], spread_scr)
            for b in range(j_dev):
                packed = packed_of(spread_scr, b)
                twice = twice_on_diagonal(packed, rows_scr.at[b])
                if first_row is not None:
                    source_row[first_row + a, b] = twice
                if first_col is not None:
                    source_col[first_col + b, a] = twice
                if first_row is not None and first_col is not None:
                    current[a * j_dev + b] = packed

        each(i_dev, step)

    if "coup" not in SKIP:
        sources(0, amplitudes, i_dev, j_dev)
        sources(0, halo.at[0], 0, None)
        sources(0, halo.at[1], 2 * i_dev, None)
        sources(0, halo.at[2], None, 0)
        sources(0, halo.at[3], None, 2 * j_dev)

    for i in range(i_dev):
        load_inter(i).wait()

    def couple(index):
        i, j = lax.div(index, j_dev), lax.rem(index, j_dev)
        spread(inter[i, j], spread_scr)
        halves, squares = [], []
        for n in range(2 * PARTNERS):
            packed = packed_of(spread_scr, n)
            if n < PARTNERS:
                orbital = row * i_dev + i
                near = jnp.clip(fock_partner[orbital, n] - (row - 1) * i_dev, 0, 3 * i_dev - 1)
                partner = source_row[near, j]
                weight = fock_value[orbital, n]
            else:
                orbital = col * j_dev + j
                near = jnp.clip(
                    fock_partner[orbital, n - PARTNERS] - (col - 1) * j_dev, 0, 3 * j_dev - 1
                )
                partner = source_col[near, i]
                weight = fock_value[orbital, n - PARTNERS]
            half = jnp.dot(packed.astype(BF16), partner, preferred_element_type=F32)
            halves.append((half * weight).astype(BF16))
            squares.append(split_twice(packed))
        coupled[index] = lax.dot_general(
            jnp.concatenate(halves, axis=1),
            jnp.concatenate(squares, axis=1),
            (((1,), (1,)), ((), ())),
            preferred_element_type=F32,
        )

    if "coup" not in SKIP:
        each(i_dev * j_dev, couple)

    pick_from = lax.broadcasted_iota(jnp.int32, (LANES, LANES), 0)
    pick_to = lax.broadcasted_iota(jnp.int32, (LANES, LANES), 1)
    from_half, from_place = pick_from // NPNO, pick_from % NPNO
    ordered = from_half * NPNO + 2 * (from_place % (NPNO // 2)) + from_place // (NPNO // 2)
    order = jnp.where(ordered == pick_to, 1.0, 0.0).astype(BF16)
    at_row = 2 * lax.broadcasted_iota(jnp.int32, (CHUNKS, LANES), 0)
    at_lane = lax.broadcasted_iota(jnp.int32, (CHUNKS, LANES), 1)
    low = at_lane < NPNO
    level_a = at_row + jnp.where(low, 0, 1)
    level_b = jnp.where(low, at_lane, at_lane - NPNO)

    def local_part(index):
        i, j = lax.div(index, j_dev), lax.rem(index, j_dev)
        sums = coupled[index]
        high = sums.astype(BF16)
        rest = (sums - high.astype(F32)).astype(BF16)
        coupling = jnp.dot(high, order, preferred_element_type=F32) + jnp.dot(
            rest, order, preferred_element_type=F32
        )
        along = energies[pl.ds(index, 1), :]
        at_b = jnp.broadcast_to(along, (CHUNKS, LANES))
        even = jnp.sum(jnp.where(at_lane == at_row, at_b, 0.0), axis=1, keepdims=True)
        odd = jnp.sum(jnp.where(at_lane == at_row + 1, at_b, 0.0), axis=1, keepdims=True)
        shift = at_b + jnp.where(low, even, odd)
        shift = shift - occupied[row * i_dev + i] - occupied[col * j_dev + j]
        coupled[index] = shift * current[index] - coupling

    if "coup" not in SKIP:
        each(i_dev * j_dev, local_part)

    def share(step):
        source = peer(step)
        arrived(row_all.at[source], gathered_row_sem.at[source])
        share_row(source).start()

    each(cols // 2 - 1, share)

    def from_sibling(step):
        source = lax.rem(sibling + 2 * step, cols)
        arrived(row_all.at[source], gathered_row_sem.at[source])

    each(cols // 2, from_sibling)

    def build(held, one, owner, slot):
        packed = held[:, slot].reshape(PAO, HALF)
        source, place = wanted(owner, slot)
        lines = one[source, per_dev].astype(F32)
        first_line = jnp.where(place == 0, lines[0:1], lines[2:3])
        last_line = jnp.where(place == 0, lines[1:2], lines[3:4])
        triangles = packed[:HALF].astype(F32)
        turned = jnp.transpose(triangles)
        cross = packed[HALF:].astype(F32)
        first = jnp.where(lower, triangles, jnp.where(upper, turned, first_line))
        last = jnp.where(upper, triangles, jnp.where(lower, turned, last_line))
        metric[slot, :HALF, :HALF] = first.astype(BF16)
        metric[slot, :HALF, HALF:] = cross.astype(BF16)
        metric[slot, HALF:, :HALF] = jnp.transpose(cross).astype(BF16)
        metric[slot, HALF:, HALF:] = last.astype(BF16)

    def contract(left, right, total):
        def step(i):
            pieces = []
            for s in range(DOMAIN):
                slot = DOMAIN * i + s
                mapped = jnp.dot(metric[slot], right[slot], preferred_element_type=F32)
                pieces.append(
                    jnp.dot(left[slot], mapped.astype(BF16), preferred_element_type=F32)
                )
            whole = pieces[0] + pieces[1] + pieces[2]
            total[i, 0] = whole[:, :LANES]
            total[i, 1] = whole[:, LANES:]

        each(i_dev, step)

    def build_all(held, one, owner):
        def step(i):
            for s in range(DOMAIN):
                build(held, one, owner, DOMAIN * i + s)

        each(i_dev, step)

    if "build" not in SKIP:
        build_all(row_all, row_one, row)
    if "dots" not in SKIP:
        contract(left_row, right_row, total_row)

    each(rows, lambda source: arrived(col_all.at[source], gathered_col_sem.at[source]))

    if "build" not in SKIP:
        build_all(col_all, col_one, col)
    if "dots" not in SKIP:
        contract(left_col, right_col, total_col)

    def square_of(total, outer, inner):
        window = total.at[outer, inner // 2]
        even = window[pl.ds(NPNO * inner, CHUNKS, stride=2), :]
        odd = window[pl.ds(NPNO * inner + 1, CHUNKS, stride=2), :]
        if inner % 2 == 0:
            return jnp.where(low, even, swap_halves(odd))
        return jnp.where(low, swap_halves(even), odd)

    level = jnp.maximum(level_a, level_b)
    for i in range(i_dev):
        for j in range(j_dev):
            both = square_of(total_row, i, j) + square_of(total_col, j, i)
            result = both * (2 * DOMAIN * AUX) ** (-0.5) + coupled[i * j_dev + j]
            result = jnp.where(level < kept[i, j], result, 0.0)
            spread_scr[pl.ds(j, CHUNKS, stride=SUB), :] = result
        for k in range(CHUNKS):
            out_ref[i, :, LANES * k : LANES * k + LANES] = spread_scr[SUB * k : SUB * k + j_dev, :]

    def finish(step):
        to_plane(other_row(step)).wait_send()
        to_row(other_col(step)).wait_send()
        gather_col(other_row(step)).wait_send()
        to_col(other_col(step)).wait_send()

    each(rows - 1, finish)
    for place in range(4):
        to_halo(place).wait_send()
    gather_row(sibling).wait_send()
    each(cols // 2 - 1, lambda step: gather_row(peer(step)).wait_send())
    each(cols // 2 - 1, lambda step: share_row(peer(step)).wait_send())


def on_device(
    fitting,
    coefficients,
    amplitudes,
    intersections,
    virtual_energy,
    occupied_energy,
    kept_count,
    orbital_atoms,
    fock_partner,
    fock_value,
):
    rows = lax.axis_size("row")
    cols = lax.axis_size("col")
    i_dev, j_dev = coefficients.shape[:2]
    per_dev = fitting.shape[0]
    slots = i_dev * DOMAIN
    pairs = i_dev * j_dev
    energies = virtual_energy.reshape(pairs, NPNO)
    energies = jnp.concatenate([energies, energies], axis=1)

    def body(*refs):
        residual_kernel(rows, cols, i_dev, j_dev, per_dev, *refs)

    dma = pltpu.SemaphoreType.DMA
    slices = (per_dev + 1, 16, HALF)
    smem = pl.BlockSpec(memory_space=pltpu.SMEM)
    vmem = pl.BlockSpec(memory_space=pltpu.VMEM)
    hbm = pl.BlockSpec(memory_space=pl.ANY)
    return pl.pallas_call(
        body,
        out_shape=jax.ShapeDtypeStruct(amplitudes.shape, F32),
        in_specs=[smem] * 5 + [vmem] * 3 + [hbm] * 2,
        out_specs=vmem,
        scratch_shapes=[
            pltpu.VMEM(coefficients.shape, BF16),
            pltpu.VMEM(intersections.shape, BF16),
            pltpu.VMEM((slots, PAO, PAO), BF16),
            pltpu.VMEM((slots, PAO, PAO), BF16),
            pltpu.VMEM((slots, PAO, PAO), BF16),
            pltpu.VMEM((slots, PAO, PAO), BF16),
            pltpu.VMEM((i_dev, 2, PAO, LANES), F32),
            pltpu.VMEM((j_dev, 2, PAO, LANES), F32),
            pltpu.VMEM((slots, PAO, PAO), BF16),
            pltpu.VMEM((cols,) + slices, BF16),
            pltpu.VMEM((rows,) + slices, BF16),
            pltpu.VMEM((cols,) + slices, BF16),
            pltpu.VMEM((cols,) + slices, BF16),
            pltpu.VMEM((slots, 16, HALF), BF16),
            pltpu.VMEM((cols, slots, 16, HALF), BF16),
            pltpu.VMEM((rows, slots, 16, HALF), BF16),
            pltpu.VMEM((4,) + amplitudes.shape, BF16),
            pltpu.VMEM((3 * i_dev, j_dev, LANES, LANES), BF16),
            pltpu.VMEM((3 * j_dev, i_dev, LANES, LANES), BF16),
            pltpu.VMEM((pairs, CHUNKS, LANES), F32),
            pltpu.VMEM((pairs, CHUNKS, LANES), F32),
            pltpu.VMEM((SUB * CHUNKS, LANES), F32),
            pltpu.VMEM((j_dev, NPNO, LANES), F32),
            dma((i_dev,)),
            dma((i_dev,)),
        ]
        + [dma((rows,))] * 11
        + [dma((4,))] * 2,
        compiler_params=pltpu.CompilerParams(
            collective_id=0, has_side_effects=True, vmem_limit_bytes=56 * 1024 * 1024
        ),
        name="residual",
    )(
        orbital_atoms,
        fock_partner,
        fock_value,
        occupied_energy,
        kept_count,
        fitting,
        amplitudes,
        energies,
        coefficients,
        intersections,
    )


def solution(mesh):
    placed = (
        P(("row", "col"), None, None),
        P("row", "col", None, None, None),
        P("row", "col", None),
        P("row", "col", None, None),
        P("row", "col", None),
        P(),
        P("row", "col"),
        P(),
        P(),
        P(),
    )
    return jax.shard_map(
        on_device, mesh=mesh, in_specs=placed, out_specs=P("row", "col", None), check_vma=False
    )
```

time: 127 us -> 57.1 us (0.45); the launches traced: 125 us -> 56.8 us
  Pallas kernels: 76.1 us -> 49.5 us
  local copies, waits for them, and re-layouts: 17.5 us -> 5.79 us
  starting transfers between devices: 11.3 us -> 0 us
  other arithmetic: 11.3 us -> 1.44 us
  matrix products: 8.32 us -> 0 us
    pallas_call x1, Pallas kernels: 76.1 us -> 49.5 us  [on_device(): pl.pallas_call(body, out_shape=jax.ShapeDtypeStruct(amplitudes.shape, F32...]
    ppermute x4 -> x0, starting transfers between devices: 11.3 us -> none  [passed_along(): return lax.ppermute(block, axis, route)]
    reshape x3 -> x0, local copies, waits for them, and re-layouts: 8.54 us -> none  [the longest x1 4.36 us: on_device(): jnp.concatenate([from_rows, from_columns], axis=2)]
    dot_general x2 -> x0, matrix products: 8.32 us -> none  [the longest x1 5.26 us: on_device(): jnp.einsum('ijnac,ijndc->ijnad', half, intersection_mats, preferred_eleme...]
    unnamed x12 -> x4, local copies, waits for them, and re-layouts: 1.18 us -> 5.79 us
    select_n x3 -> x0, other arithmetic: 4.42 us -> none  [the longest x1 2.17 us: on_device(): from_columns = jnp.take(column_source, column_pick, axis=1)]
    concatenate x4 -> x1, other arithmetic: 5.22 us -> 1.44 us  [on_device(): energies = jnp.concatenate([energies, energies], axis=1)]
    gather x2 -> x0, local copies, waits for them, and re-layouts: 3.51 us -> none  [the longest x1 1.76 us: on_device(): from_columns = jnp.take(column_source, column_pick, axis=1)]
  transfers between devices with their start and end apart: 4 -> 0, of which waited for: 0 -> 0; matrix products, arithmetic and copies ran while one was open for 12% -> 0% of each run, Pallas kernels for 61% -> 0%
where the time goes in v2:
time: 57.1 us; the launch traced here: 56.8 us
  Pallas kernels  49.5 us (87%)
  local copies, waits for them, and re-layouts  5.79 us (10%)
  other arithmetic  1.44 us (3%)
    pallas_call x1, Pallas kernels, on_device(): pl.pallas_call(body, out_shape=jax.ShapeDtypeStruct(amplitudes.shape, F32...  49.5 us
    unnamed x4, local copies, waits for them, and re-layouts  5.79 us
    concatenate x1, other arithmetic, on_device(): energies = jnp.concatenate([energies, energies], axis=1)  1.44 us

profile of v2, /device:TPU:1, one launch (start us, length us, event | category | flops | bytes accessed | tf_op | source)
XLA Modules:
  0.0 56.8 jit_solution(5750890023865988830)
XLA Ops:
  0.0 1.4 %pad_maximum_fusion.refs_7_ = f32[16,128]{1,0:T(8,128)} fusion(f32[16,64]{1,0:T(8,128)} %bitcast.1), kind=kLoop, calls=%fused_computation | loop fusion | flops 2048 | bytes 12288 | tf_op jit(solution)/shard_map/concatenate | solution.py:543
  1.4 1.4 %copy.11.refs_0_ = s32[64,3]{1,0:T(8,128)} copy(s32[64,3]{0,1:T(4,128)} %param.17) | data formatting | bytes 1536 | tf_op args[7]
  2.8 1.4 %copy.12.refs_1_ = s32[64,4]{1,0:T(8,128)} copy(s32[64,4]{0,1:T(4,128)} %param.18) | data formatting | bytes 2048 | tf_op args[8]
  4.2 1.4 %copy.13.refs_2_ = f32[64,4]{1,0:T(8,128)} copy(f32[64,4]{0,1:T(4,128)} %param.19) | data formatting | bytes 2048 | tf_op args[9]
  5.6 49.5 %residual.1 = f32[4,4,4096]{2,1,0:T(4,128)} custom-call(s32[64,3]{1,0:T(8,128)} %copy.11.refs_0_, s32[64,4]{1,0:T(8,128)} %copy.12.refs_1_, f32[64,4]{1,0:T(8,128)} %copy.13.refs_2_, f32[64]{0:T(128)} %refs_3_.1, s32[4,4]{1,0:T(4,128)} %refs_4_.1, bf16[2,512,256]{2,1,0:T(8,128)(2,1)} %refs_5_.1, bf16[4,4,4096]{2,1,0:T(4,128)(2,1)} %refs_6_.1, ...), custom_call_target="tpu_custom_call" | custom-call | tf_op jit(solution)/shard_map/residual/pallas_call | solution.py:553
  55.1 1.7 %copy.15 = f32[4,4,4096]{2,1,0:T(4,128)} copy(f32[4,4,4096]{2,1,0:T(4,128)} %residual.1) | data formatting | bytes 524288

commit v3 on v2

--- a/solution.py
+++ b/solution.py
@@ -18,6 +18,8 @@
 
 
 SUB = 8
+EARLY_PAIRS = 4
+PARTS = 2
 LANES = 128
 PAIR = 2 * NPNO
 CHUNKS = NPNO * NPNO // LANES
@@ -102,6 +104,17 @@
     i_dev,
     j_dev,
     per_dev,
+    orbital_atoms_hbm,
+    fock_partner_hbm,
+    fock_value_hbm,
+    occupied_hbm,
+    kept_hbm,
+    fitting_hbm,
+    amplitudes_hbm,
+    energies_hbm,
+    coefficients,
+    intersections,
+    out_hbm,
     orbital_atoms,
     fock_partner,
     fock_value,
@@ -110,8 +123,6 @@
     fitting,
     amplitudes,
     energies,
-    coefficients,
-    intersections,
     out_ref,
     coef,
     inter,
@@ -151,6 +162,8 @@
     gathered_col_sem,
     send_halo_sem,
     recv_halo_sem,
+    load_sem,
+    out_sem,
 ):
     row = lax.axis_index("row")
     col = lax.axis_index("col")
@@ -171,7 +184,27 @@
             barrier, inc=1, device_id={"row": row, "col": other}, device_id_type=MESH
         )
 
+    load_fitting = pltpu.make_async_copy(fitting_hbm, fitting, load_sem.at[0])
+    load_amplitudes = pltpu.make_async_copy(amplitudes_hbm, amplitudes, load_sem.at[1])
+    load_energies = pltpu.make_async_copy(energies_hbm, energies, load_sem.at[2])
+    tables = [
+        pltpu.make_async_copy(source, table, load_sem.at[3 + k])
+        for k, (source, table) in enumerate(
+            (
+                (orbital_atoms_hbm, orbital_atoms),
+                (fock_partner_hbm, fock_partner),
+                (fock_value_hbm, fock_value),
+                (occupied_hbm, occupied),
+                (kept_hbm, kept),
+            )
+        )
+    ]
+    load_fitting.start()
     each(rows - 1, greet)
+    for table in tables:
+        table.start()
+    load_amplitudes.start()
+    load_energies.start()
 
     def load_coef(i):
         return pltpu.make_async_copy(coefficients.at[i], coef.at[i], coef_sem.at[i])
@@ -191,6 +224,11 @@
     on = above == across
     tile_row = lax.broadcasted_iota(jnp.int32, (16, HALF), 0)
     diagonal = jnp.zeros((16, HALF), F32)
+    load_fitting.wait()
+    load_amplitudes.wait()
+    load_energies.wait()
+    for table in tables:
+        table.wait()
     for a in range(per_dev):
         block = fitting[a]
         square = lax.dot_general(
@@ -273,6 +311,7 @@
         load_coef(i).wait()
     if "turn" not in SKIP:
         each(slots, order_row)
+        each(slots, order_col)
 
     def pass_on(step):
         other = other_row(step)
@@ -292,7 +331,7 @@
 
     def wanted(owner, slot):
         orbital = owner * i_dev + lax.div(slot, DOMAIN)
-        atom = orbital_atoms[orbital, lax.rem(slot, DOMAIN)] - owner * row_atoms
+        atom = orbital_atoms[lax.rem(slot, DOMAIN), orbital] - owner * row_atoms
         atom = jnp.clip(atom, 0, row_atoms - 1)
         return lax.div(atom, per_dev), lax.rem(atom, per_dev)
 
@@ -302,40 +341,30 @@
 
     each(slots, pick_row)
 
-    def gather_row(other):
+    def part_of(ref, part):
+        return ref.at[pl.ds(part * (slots // PARTS), slots // PARTS)]
+
+    def gather_row(part, other):
+        held = part_of(row_all.at[col], part)
         return remote(
-            row_all.at[col], row_all.at[col], gather_row_sem.at[other], gathered_row_sem.at[col], row, other
-        )
-
-    def share_row(source):
+            held, held, gather_row_sem.at[part, other], gathered_row_sem.at[part, col], row, other
+        )
+
+    def share_row(part, source):
+        held = part_of(row_all.at[source], part)
         return remote(
-            row_all.at[source], row_all.at[source], share_sem.at[source], gathered_row_sem.at[source], row, sibling
-        )
+            held, held, share_sem.at[part, source], gathered_row_sem.at[part, source], row, sibling
+        )
+
+    def row_arrived(part, source):
+        arrived(part_of(row_all.at[source], part), gathered_row_sem.at[part, source])
 
     def peer(step):
         return lax.rem(col + 2 * (step + 1), cols)
 
-    each(cols // 2 - 1, lambda step: gather_row(peer(step)).start())
-    gather_row(sibling).start()
-
-    if "turn" not in SKIP:
-        each(slots, order_col)
-
-    each(cols, lambda source: arrived(col_one.at[source], recv_col_sem.at[source]))
-
-    def pick_col(slot):
-        source, place = wanted(col, slot)
-        col_pick[slot] = col_one[source, place]
-
-    each(slots, pick_col)
-
-    def gather_col(other):
-        return remote(
-            col_pick, col_all.at[row], gather_col_sem.at[other], gathered_col_sem.at[row], other, col
-        )
-
-    each(rows - 1, lambda step: gather_col(other_row(step)).start())
-    pltpu.make_async_copy(col_pick, col_all.at[row], gathered_col_sem.at[row]).start()
+    for part in range(PARTS):
+        each(cols // 2 - 1, lambda step: gather_row(part, peer(step)).start())
+        gather_row(part, sibling).start()
 
     for place in range(4):
         arrived(halo.at[place], recv_halo_sem.at[place])
@@ -373,16 +402,16 @@
             packed = packed_of(spread_scr, n)
             if n < PARTNERS:
                 orbital = row * i_dev + i
-                near = jnp.clip(fock_partner[orbital, n] - (row - 1) * i_dev, 0, 3 * i_dev - 1)
+                near = jnp.clip(fock_partner[n, orbital] - (row - 1) * i_dev, 0, 3 * i_dev - 1)
                 partner = source_row[near, j]
-                weight = fock_value[orbital, n]
+                weight = fock_value[n, orbital]
             else:
                 orbital = col * j_dev + j
                 near = jnp.clip(
-                    fock_partner[orbital, n - PARTNERS] - (col - 1) * j_dev, 0, 3 * j_dev - 1
+                    fock_partner[n - PARTNERS, orbital] - (col - 1) * j_dev, 0, 3 * j_dev - 1
                 )
                 partner = source_col[near, i]
-                weight = fock_value[orbital, n - PARTNERS]
+                weight = fock_value[n - PARTNERS, orbital]
             half = jnp.dot(packed.astype(BF16), partner, preferred_element_type=F32)
             halves.append((half * weight).astype(BF16))
             squares.append(split_twice(packed))
@@ -394,7 +423,40 @@
         )
 
     if "coup" not in SKIP:
-        each(i_dev * j_dev, couple)
+        each(EARLY_PAIRS, couple)
+
+    each(cols, lambda source: arrived(col_one.at[source], recv_col_sem.at[source]))
+
+    def pick_col(slot):
+        source, place = wanted(col, slot)
+        col_pick[slot] = col_one[source, place]
+
+    each(slots, pick_col)
+
+    def gather_col(part, other):
+        return remote(
+            part_of(col_pick, part),
+            part_of(col_all.at[row], part),
+            gather_col_sem.at[part, other],
+            gathered_col_sem.at[part, row],
+            other,
+            col,
+        )
+
+    def keep_col(part):
+        return pltpu.make_async_copy(
+            part_of(col_pick, part), part_of(col_all.at[row], part), gathered_col_sem.at[part, row]
+        )
+
+    def col_arrived(part, source):
+        arrived(part_of(col_all.at[source], part), gathered_col_sem.at[part, source])
+
+    for part in range(PARTS):
+        each(rows - 1, lambda step: gather_col(part, other_row(step)).start())
+        keep_col(part).start()
+
+    if "coup" not in SKIP:
+        each(i_dev * j_dev - EARLY_PAIRS, lambda index: couple(index + EARLY_PAIRS))
 
     pick_from = lax.broadcasted_iota(jnp.int32, (LANES, LANES), 0)
     pick_to = lax.broadcasted_iota(jnp.int32, (LANES, LANES), 1)
@@ -407,37 +469,39 @@
     level_a = at_row + jnp.where(low, 0, 1)
     level_b = jnp.where(low, at_lane, at_lane - NPNO)
 
-    def local_part(index):
-        i, j = lax.div(index, j_dev), lax.rem(index, j_dev)
+    def local_part(i, j, along):
+        index = i * j_dev + j
         sums = coupled[index]
         high = sums.astype(BF16)
         rest = (sums - high.astype(F32)).astype(BF16)
         coupling = jnp.dot(high, order, preferred_element_type=F32) + jnp.dot(
             rest, order, preferred_element_type=F32
         )
-        along = energies[pl.ds(index, 1), :]
-        at_b = jnp.broadcast_to(along, (CHUNKS, LANES))
+        at_b = jnp.broadcast_to(jnp.concatenate([along, along], axis=1), (CHUNKS, LANES))
         even = jnp.sum(jnp.where(at_lane == at_row, at_b, 0.0), axis=1, keepdims=True)
         odd = jnp.sum(jnp.where(at_lane == at_row + 1, at_b, 0.0), axis=1, keepdims=True)
         shift = at_b + jnp.where(low, even, odd)
         shift = shift - occupied[row * i_dev + i] - occupied[col * j_dev + j]
         coupled[index] = shift * current[index] - coupling
 
+    def local_row(i):
+        levels = energies[i]
+        for j in range(j_dev):
+            local_part(i, j, levels[j : j + 1])
+
     if "coup" not in SKIP:
-        each(i_dev * j_dev, local_part)
-
-    def share(step):
-        source = peer(step)
-        arrived(row_all.at[source], gathered_row_sem.at[source])
-        share_row(source).start()
-
-    each(cols // 2 - 1, share)
-
-    def from_sibling(step):
-        source = lax.rem(sibling + 2 * step, cols)
-        arrived(row_all.at[source], gathered_row_sem.at[source])
-
-    each(cols // 2, from_sibling)
+        each(i_dev, local_row)
+
+    def share(part):
+        def step(number):
+            source = peer(number)
+            row_arrived(part, source)
+            share_row(part, source).start()
+
+        each(cols // 2 - 1, step)
+
+    def from_sibling(part):
+        each(cols // 2, lambda step: row_arrived(part, lax.rem(sibling + 2 * step, cols)))
 
     def build(held, one, owner, slot):
         packed = held[:, slot].reshape(PAO, HALF)
@@ -455,7 +519,7 @@
         metric[slot, HALF:, :HALF] = jnp.transpose(cross).astype(BF16)
         metric[slot, HALF:, HALF:] = last.astype(BF16)
 
-    def contract(left, right, total):
+    def contract(part, left, right, total):
         def step(i):
             pieces = []
             for s in range(DOMAIN):
@@ -468,26 +532,29 @@
             total[i, 0] = whole[:, :LANES]
             total[i, 1] = whole[:, LANES:]
 
-        each(i_dev, step)
-
-    def build_all(held, one, owner):
+        each(i_dev // PARTS, lambda i: step(i + part * (i_dev // PARTS)))
+
+    def build_all(part, held, one, owner):
         def step(i):
             for s in range(DOMAIN):
                 build(held, one, owner, DOMAIN * i + s)
 
-        each(i_dev, step)
-
-    if "build" not in SKIP:
-        build_all(row_all, row_one, row)
-    if "dots" not in SKIP:
-        contract(left_row, right_row, total_row)
-
-    each(rows, lambda source: arrived(col_all.at[source], gathered_col_sem.at[source]))
-
-    if "build" not in SKIP:
-        build_all(col_all, col_one, col)
-    if "dots" not in SKIP:
-        contract(left_col, right_col, total_col)
+        each(i_dev // PARTS, lambda i: step(i + part * (i_dev // PARTS)))
+
+    for part in range(PARTS):
+        share(part)
+    for part in range(PARTS):
+        from_sibling(part)
+        if "build" not in SKIP:
+            build_all(part, row_all, row_one, row)
+        if "dots" not in SKIP:
+            contract(part, left_row, right_row, total_row)
+    for part in range(PARTS):
+        each(rows, lambda source: col_arrived(part, source))
+        if "build" not in SKIP:
+            build_all(part, col_all, col_one, col)
+        if "dots" not in SKIP:
+            contract(part, left_col, right_col, total_col)
 
     def square_of(total, outer, inner):
         window = total.at[outer, inner // 2]
@@ -496,6 +563,9 @@
         if inner % 2 == 0:
             return jnp.where(low, even, swap_halves(odd))
         return jnp.where(low, swap_halves(even), odd)
+
+    def store_out(i):
+        return pltpu.make_async_copy(out_ref.at[i], out_hbm.at[i], out_sem.at[i])
 
     level = jnp.maximum(level_a, level_b)
     for i in range(i_dev):
@@ -506,19 +576,29 @@
             spread_scr[pl.ds(j, CHUNKS, stride=SUB), :] = result
         for k in range(CHUNKS):
             out_ref[i, :, LANES * k : LANES * k + LANES] = spread_scr[SUB * k : SUB * k + j_dev, :]
+        store_out(i).start()
 
     def finish(step):
         to_plane(other_row(step)).wait_send()
         to_row(other_col(step)).wait_send()
-        gather_col(other_row(step)).wait_send()
+        for part in range(PARTS):
+            gather_col(part, other_row(step)).wait_send()
         to_col(other_col(step)).wait_send()
 
     each(rows - 1, finish)
+    for i in range(i_dev):
+        store_out(i).wait()
     for place in range(4):
         to_halo(place).wait_send()
-    gather_row(sibling).wait_send()
-    each(cols // 2 - 1, lambda step: gather_row(peer(step)).wait_send())
-    each(cols // 2 - 1, lambda step: share_row(peer(step)).wait_send())
+    for part in range(PARTS):
+        gather_row(part, sibling).wait_send()
+
+    def finish_row(step):
+        for part in range(PARTS):
+            gather_row(part, peer(step)).wait_send()
+            share_row(part, peer(step)).wait_send()
+
+    each(cols // 2 - 1, finish_row)
 
 
 def on_device(
@@ -539,23 +619,28 @@
     per_dev = fitting.shape[0]
     slots = i_dev * DOMAIN
     pairs = i_dev * j_dev
-    energies = virtual_energy.reshape(pairs, NPNO)
-    energies = jnp.concatenate([energies, energies], axis=1)
 
     def body(*refs):
         residual_kernel(rows, cols, i_dev, j_dev, per_dev, *refs)
 
     dma = pltpu.SemaphoreType.DMA
     slices = (per_dev + 1, 16, HALF)
-    smem = pl.BlockSpec(memory_space=pltpu.SMEM)
-    vmem = pl.BlockSpec(memory_space=pltpu.VMEM)
     hbm = pl.BlockSpec(memory_space=pl.ANY)
     return pl.pallas_call(
         body,
         out_shape=jax.ShapeDtypeStruct(amplitudes.shape, F32),
-        in_specs=[smem] * 5 + [vmem] * 3 + [hbm] * 2,
-        out_specs=vmem,
+        in_specs=[hbm] * 10,
+        out_specs=hbm,
         scratch_shapes=[
+            pltpu.SMEM(orbital_atoms.shape[::-1], jnp.int32),
+            pltpu.SMEM(fock_partner.shape[::-1], jnp.int32),
+            pltpu.SMEM(fock_value.shape[::-1], F32),
+            pltpu.SMEM(occupied_energy.shape, F32),
+            pltpu.SMEM(kept_count.shape, jnp.int32),
+            pltpu.VMEM(fitting.shape, BF16),
+            pltpu.VMEM(amplitudes.shape, BF16),
+            pltpu.VMEM(virtual_energy.shape, F32),
+            pltpu.VMEM(amplitudes.shape, F32),
             pltpu.VMEM(coefficients.shape, BF16),
             pltpu.VMEM(intersections.shape, BF16),
             pltpu.VMEM((slots, PAO, PAO), BF16),
@@ -582,21 +667,23 @@
             dma((i_dev,)),
             dma((i_dev,)),
         ]
-        + [dma((rows,))] * 11
-        + [dma((4,))] * 2,
+        + [dma((rows,))] * 6
+        + [dma((PARTS, rows))] * 5
+        + [dma((4,))] * 2
+        + [dma((8,)), dma((i_dev,))],
         compiler_params=pltpu.CompilerParams(
-            collective_id=0, has_side_effects=True, vmem_limit_bytes=56 * 1024 * 1024
+            collective_id=0, has_side_effects=True, vmem_limit_bytes=62 * 1024 * 1024
         ),
         name="residual",
     )(
-        orbital_atoms,
-        fock_partner,
-        fock_value,
+        orbital_atoms.T,
+        fock_partner.T,
+        fock_value.T,
         occupied_energy,
         kept_count,
         fitting,
         amplitudes,
-        energies,
+        virtual_energy,
         coefficients,
         intersections,
     )

time: 57.1 us -> 43.7 us (0.77)
  Pallas kernels: 49.5 us -> 41.9 us
  local copies, waits for them, and re-layouts: 5.79 us -> 1.67 us
  other arithmetic: 1.44 us -> 0 us
    pallas_call x1, Pallas kernels: 49.5 us -> 41.9 us  [on_device(): pl.pallas_call(body, out_shape=jax.ShapeDtypeStruct(amplitudes.shape, F32...]
    unnamed x4 -> x1, local copies, waits for them, and re-layouts: 5.79 us -> 1.67 us
    concatenate x1 -> x0, other arithmetic: 1.44 us -> none  [on_device(): energies = jnp.concatenate([energies, energies], axis=1)]
where the time goes in v3:
time: 43.7 us; the launch traced here: 43.6 us
  Pallas kernels  41.9 us (96%)
  local copies, waits for them, and re-layouts  1.67 us (4%)
    pallas_call x1, Pallas kernels, on_device(): pl.pallas_call(body, out_shape=jax.ShapeDtypeStruct(amplitudes.shape, F32...  41.9 us
    unnamed x1, local copies, waits for them, and re-layouts  1.67 us

profile of v3, /device:TPU:1, one launch (start us, length us, event | category | flops | bytes accessed | tf_op | source)
XLA Modules:
  0.0 43.6 jit_solution(7633294890024737631)
XLA Ops:
  0.0 41.9 %residual.1 = f32[4,4,4096]{2,1,0:T(4,128)} custom-call(s32[3,64]{1,0:T(4,128)} %bitcast.3, s32[4,64]{1,0:T(4,128)} %bitcast.4, f32[4,64]{1,0:T(4,128)} %bitcast.5, f32[64]{0:T(128)} %refs_3_.1, s32[4,4]{1,0:T(4,128)} %refs_4_.1, bf16[2,512,256]{2,1,0:T(8,128)(2,1)} %refs_5_.1, bf16[4,4,4096]{2,1,0:T(4,128)(2,1)} %refs_6_.1, f32[4,4,64]{2,1,0:T(4,128)} %refs_7_.1, ...), custom_call_target="tpu_custom_call" | custom-call | tf_op jit(solution)/shard_map/residual/pallas_call | solution.py:629
  41.9 1.7 %copy.12 = f32[4,4,4096]{2,1,0:T(4,128)} copy(f32[4,4,4096]{2,1,0:T(4,128)} %residual.1) | data formatting | bytes 524288

commit v4 on v3

--- a/solution.py
+++ b/solution.py
@@ -20,6 +20,7 @@
 SUB = 8
 EARLY_PAIRS = 4
 PARTS = 2
+PREPARED = 16
 LANES = 128
 PAIR = 2 * NPNO
 CHUNKS = NPNO * NPNO // LANES
@@ -46,6 +47,14 @@
         return carry
 
     lax.fori_loop(0, count, step, 0)
+
+
+def twice(count, body):
+    def step(index):
+        body(2 * index)
+        body(2 * index + 1)
+
+    each(count // 2, step)
 
 
 def swap_halves(value):
@@ -147,6 +156,11 @@
     coupled,
     spread_scr,
     rows_scr,
+    lines_row,
+    lines_col,
+    flats,
+    squares,
+    more_scr,
     coef_sem,
     inter_sem,
     send_row_sem,
@@ -164,6 +178,8 @@
     recv_halo_sem,
     load_sem,
     out_sem,
+    send_lines_sem,
+    recv_lines_sem,
 ):
     row = lax.axis_index("row")
     col = lax.axis_index("col")
@@ -236,14 +252,13 @@
         )
         first = square[:HALF, :HALF]
         last = square[HALF:, HALF:]
-        triangles = jnp.where(lower, first, jnp.where(upper, last, 0.0)).astype(BF16)
+        triangles = jnp.where(upper, last, first).astype(BF16)
         cross = square[:HALF, HALF:].astype(BF16)
         for d in range(cols // 2):
             send_one[d, a] = triangles[16 * d : 16 * d + 16]
             send_one[cols // 2 + d, a] = cross[16 * d : 16 * d + 16]
-        for part, piece in ((0, first), (1, last)):
-            line = jnp.sum(jnp.where(on, piece, 0.0), axis=0, keepdims=True)
-            diagonal = jnp.where(tile_row == 2 * a + part, line, diagonal)
+        line = jnp.sum(jnp.where(on, last, 0.0), axis=0, keepdims=True)
+        diagonal = jnp.where(tile_row == a, line, diagonal)
     for d in range(cols):
         send_one[d, per_dev] = diagonal.astype(BF16)
 
@@ -251,7 +266,7 @@
 
     def to_plane(other):
         return remote(
-            send_one.at[other], relay.at[row], send_relay_sem.at[other], recv_relay_sem.at[row], other, col
+            send_one.at[other, pl.ds(0, per_dev)], relay.at[row], send_relay_sem.at[other], recv_relay_sem.at[row], other, col
         )
 
     def to_row(other):
@@ -282,7 +297,9 @@
         to_row(other_col(step)).start()
 
     each(rows - 1, start_first)
-    pltpu.make_async_copy(send_one.at[row], relay.at[row], recv_relay_sem.at[row]).start()
+    pltpu.make_async_copy(
+        send_one.at[row, pl.ds(0, per_dev)], relay.at[row], recv_relay_sem.at[row]
+    ).start()
     pltpu.make_async_copy(send_one.at[col], row_one.at[col], recv_row_sem.at[col]).start()
     for place in range(4):
         to_halo(place).start()
@@ -313,6 +330,20 @@
         each(slots, order_row)
         each(slots, order_col)
 
+    for i in range(i_dev):
+        load_inter(i).wait()
+
+    def prepare(index):
+        scratch = more_scr.at[lax.rem(index, 2)]
+        spread(inter[lax.div(index, j_dev), lax.rem(index, j_dev)], scratch)
+        for n in range(2 * PARTNERS):
+            packed = packed_of(scratch, n)
+            flats[index, n] = packed.astype(BF16)
+            squares[index, n] = split_twice(packed)
+
+    if "coup" not in SKIP:
+        twice(PREPARED, prepare)
+
     def pass_on(step):
         other = other_row(step)
         arrived(relay.at[other], recv_relay_sem.at[other])
@@ -340,6 +371,23 @@
         row_all[col, slot] = row_one[source, place]
 
     each(slots, pick_row)
+    lines = jnp.zeros((16, HALF), F32)
+    for slot in range(slots):
+        source, place = wanted(row, slot)
+        tile = row_one[source, per_dev].astype(F32)
+        line = tile[0:1]
+        for a in range(1, per_dev):
+            line = jnp.where(place == a, tile[a : a + 1], line)
+        lines = jnp.where(tile_row == slot, line, lines)
+    lines_row[...] = lines
+
+    def send_lines(other):
+        return remote(lines_row, lines_col, send_lines_sem.at[other], recv_lines_sem.at[0], other, col)
+
+    @pl.when(row == col)
+    def _():
+        each(rows - 1, lambda step: send_lines(other_row(step)).start())
+        pltpu.make_async_copy(lines_row, lines_col, recv_lines_sem.at[0]).start()
 
     def part_of(ref, part):
         return ref.at[pl.ds(part * (slots // PARTS), slots // PARTS)]
@@ -365,6 +413,9 @@
     for part in range(PARTS):
         each(cols // 2 - 1, lambda step: gather_row(part, peer(step)).start())
         gather_row(part, sibling).start()
+
+    if "coup" not in SKIP:
+        each(i_dev * j_dev - PREPARED, lambda index: prepare(index + PREPARED))
 
     for place in range(4):
         arrived(halo.at[place], recv_halo_sem.at[place])
@@ -374,11 +425,11 @@
             spread(block[a], spread_scr)
             for b in range(j_dev):
                 packed = packed_of(spread_scr, b)
-                twice = twice_on_diagonal(packed, rows_scr.at[b])
+                doubled = twice_on_diagonal(packed, rows_scr.at[b])
                 if first_row is not None:
-                    source_row[first_row + a, b] = twice
+                    source_row[first_row + a, b] = doubled
                 if first_col is not None:
-                    source_col[first_col + b, a] = twice
+                    source_col[first_col + b, a] = doubled
                 if first_row is not None and first_col is not None:
                     current[a * j_dev + b] = packed
 
@@ -391,15 +442,10 @@
         sources(0, halo.at[2], None, 0)
         sources(0, halo.at[3], None, 2 * j_dev)
 
-    for i in range(i_dev):
-        load_inter(i).wait()
-
     def couple(index):
         i, j = lax.div(index, j_dev), lax.rem(index, j_dev)
-        spread(inter[i, j], spread_scr)
-        halves, squares = [], []
+        halves = []
         for n in range(2 * PARTNERS):
-            packed = packed_of(spread_scr, n)
             if n < PARTNERS:
                 orbital = row * i_dev + i
                 near = jnp.clip(fock_partner[n, orbital] - (row - 1) * i_dev, 0, 3 * i_dev - 1)
@@ -412,18 +458,17 @@
                 )
                 partner = source_col[near, i]
                 weight = fock_value[n - PARTNERS, orbital]
-            half = jnp.dot(packed.astype(BF16), partner, preferred_element_type=F32)
+            half = jnp.dot(flats[index, n], partner, preferred_element_type=F32)
             halves.append((half * weight).astype(BF16))
-            squares.append(split_twice(packed))
         coupled[index] = lax.dot_general(
             jnp.concatenate(halves, axis=1),
-            jnp.concatenate(squares, axis=1),
+            jnp.concatenate([squares[index, n] for n in range(2 * PARTNERS)], axis=1),
             (((1,), (1,)), ((), ())),
             preferred_element_type=F32,
         )
 
     if "coup" not in SKIP:
-        each(EARLY_PAIRS, couple)
+        twice(EARLY_PAIRS, couple)
 
     each(cols, lambda source: arrived(col_one.at[source], recv_col_sem.at[source]))
 
@@ -456,7 +501,7 @@
         keep_col(part).start()
 
     if "coup" not in SKIP:
-        each(i_dev * j_dev - EARLY_PAIRS, lambda index: couple(index + EARLY_PAIRS))
+        twice(i_dev * j_dev - EARLY_PAIRS, lambda index: couple(index + EARLY_PAIRS))
 
     pick_from = lax.broadcasted_iota(jnp.int32, (LANES, LANES), 0)
     pick_to = lax.broadcasted_iota(jnp.int32, (LANES, LANES), 1)
@@ -503,16 +548,13 @@
     def from_sibling(part):
         each(cols // 2, lambda step: row_arrived(part, lax.rem(sibling + 2 * step, cols)))
 
-    def build(held, one, owner, slot):
+    def build(held, lines, slot):
         packed = held[:, slot].reshape(PAO, HALF)
-        source, place = wanted(owner, slot)
-        lines = one[source, per_dev].astype(F32)
-        first_line = jnp.where(place == 0, lines[0:1], lines[2:3])
-        last_line = jnp.where(place == 0, lines[1:2], lines[3:4])
+        last_line = lines[pl.ds(slot, 1), :]
         triangles = packed[:HALF].astype(F32)
         turned = jnp.transpose(triangles)
         cross = packed[HALF:].astype(F32)
-        first = jnp.where(lower, triangles, jnp.where(upper, turned, first_line))
+        first = jnp.where(upper, turned, triangles)
         last = jnp.where(upper, triangles, jnp.where(lower, turned, last_line))
         metric[slot, :HALF, :HALF] = first.astype(BF16)
         metric[slot, :HALF, HALF:] = cross.astype(BF16)
@@ -532,27 +574,30 @@
             total[i, 0] = whole[:, :LANES]
             total[i, 1] = whole[:, LANES:]
 
-        each(i_dev // PARTS, lambda i: step(i + part * (i_dev // PARTS)))
-
-    def build_all(part, held, one, owner):
+        for i in range(i_dev // PARTS):
+            step(i + part * (i_dev // PARTS))
+
+    def build_all(part, held, lines):
         def step(i):
             for s in range(DOMAIN):
-                build(held, one, owner, DOMAIN * i + s)
-
-        each(i_dev // PARTS, lambda i: step(i + part * (i_dev // PARTS)))
+                build(held, lines, DOMAIN * i + s)
+
+        for i in range(i_dev // PARTS):
+            step(i + part * (i_dev // PARTS))
 
     for part in range(PARTS):
         share(part)
     for part in range(PARTS):
         from_sibling(part)
         if "build" not in SKIP:
-            build_all(part, row_all, row_one, row)
+            build_all(part, row_all, lines_row)
         if "dots" not in SKIP:
             contract(part, left_row, right_row, total_row)
+    arrived(lines_col, recv_lines_sem.at[0])
     for part in range(PARTS):
         each(rows, lambda source: col_arrived(part, source))
         if "build" not in SKIP:
-            build_all(part, col_all, col_one, col)
+            build_all(part, col_all, lines_col)
         if "dots" not in SKIP:
             contract(part, left_col, right_col, total_col)
 
@@ -599,6 +644,10 @@
             share_row(part, peer(step)).wait_send()
 
     each(cols // 2 - 1, finish_row)
+
+    @pl.when(row == col)
+    def _():
+        each(rows - 1, lambda step: send_lines(other_row(step)).wait_send())
 
 
 def on_device(
@@ -651,9 +700,9 @@
             pltpu.VMEM((j_dev, 2, PAO, LANES), F32),
             pltpu.VMEM((slots, PAO, PAO), BF16),
             pltpu.VMEM((cols,) + slices, BF16),
-            pltpu.VMEM((rows,) + slices, BF16),
+            pltpu.VMEM((rows, per_dev, 16, HALF), BF16),
             pltpu.VMEM((cols,) + slices, BF16),
-            pltpu.VMEM((cols,) + slices, BF16),
+            pltpu.VMEM((cols, per_dev, 16, HALF), BF16),
             pltpu.VMEM((slots, 16, HALF), BF16),
             pltpu.VMEM((cols, slots, 16, HALF), BF16),
             pltpu.VMEM((rows, slots, 16, HALF), BF16),
@@ -664,13 +713,18 @@
             pltpu.VMEM((pairs, CHUNKS, LANES), F32),
             pltpu.VMEM((SUB * CHUNKS, LANES), F32),
             pltpu.VMEM((j_dev, NPNO, LANES), F32),
+            pltpu.VMEM((16, HALF), F32),
+            pltpu.VMEM((16, HALF), F32),
+            pltpu.VMEM((pairs, 2 * PARTNERS, CHUNKS, LANES), BF16),
+            pltpu.VMEM((pairs, 2 * PARTNERS, LANES, LANES), BF16),
+            pltpu.VMEM((2, SUB * CHUNKS, LANES), F32),
             dma((i_dev,)),
             dma((i_dev,)),
         ]
         + [dma((rows,))] * 6
         + [dma((PARTS, rows))] * 5
         + [dma((4,))] * 2
-        + [dma((8,)), dma((i_dev,))],
+        + [dma((8,)), dma((i_dev,)), dma((rows,)), dma((1,))],
         compiler_params=pltpu.CompilerParams(
             collective_id=0, has_side_effects=True, vmem_limit_bytes=62 * 1024 * 1024
         ),

time: 43.7 us -> 41.3 us (0.945)
  Pallas kernels: 41.9 us -> 39.5 us
    pallas_call x1, Pallas kernels: 41.9 us -> 39.5 us  [on_device(): pl.pallas_call(body, out_shape=jax.ShapeDtypeStruct(amplitudes.shape, F32...]
where the time goes in v4:
time: 41.3 us; the launch traced here: 41.2 us
  Pallas kernels  39.5 us (96%)
  local copies, waits for them, and re-layouts  1.67 us (4%)
    pallas_call x1, Pallas kernels, on_device(): pl.pallas_call(body, out_shape=jax.ShapeDtypeStruct(amplitudes.shape, F32...  39.5 us
    unnamed x1, local copies, waits for them, and re-layouts  1.67 us

profile of v4, /device:TPU:1, one launch (start us, length us, event | category | flops | bytes accessed | tf_op | source)
XLA Modules:
  0.0 41.2 jit_solution(3668438411052550807)
XLA Ops:
  0.0 39.5 %residual.1 = f32[4,4,4096]{2,1,0:T(4,128)} custom-call(s32[3,64]{1,0:T(4,128)} %bitcast.3, s32[4,64]{1,0:T(4,128)} %bitcast.4, f32[4,64]{1,0:T(4,128)} %bitcast.5, f32[64]{0:T(128)} %refs_3_.1, s32[4,4]{1,0:T(4,128)} %refs_4_.1, bf16[2,512,256]{2,1,0:T(8,128)(2,1)} %refs_5_.1, bf16[4,4,4096]{2,1,0:T(4,128)(2,1)} %refs_6_.1, f32[4,4,64]{2,1,0:T(4,128)} %refs_7_.1, ...), custom_call_target="tpu_custom_call" | custom-call | tf_op jit(solution)/shard_map/residual/pallas_call | solution.py:678
  39.5 1.7 %copy.12 = f32[4,4,4096]{2,1,0:T(4,128)} copy(f32[4,4,4096]{2,1,0:T(4,128)} %residual.1) | data formatting | bytes 524288
